TPU v7x, 512 devices: a whole 4x8x8 slice. The times are simulated.
512 devices in a mesh: dp: 64 (over z, y_hi, x), mp: 8 (over y_lo, core).
Axes of the slice: x: 4, y: 8 (y_hi: 2, y_lo: 4; y = y_hi * 4 + y_lo), z: 8, core: 2. Of those that a mesh axis runs over, the one named last changes fastest.
Arguments:
- tokens: bfloat16 [32768, 8192], P('dp', 'mp'), may hold values from -6 to 6
- upstream: bfloat16 [32768, 8192], P('dp', 'mp'), may hold values from -6 to 6
- first_factor: bfloat16 [32, 256, 256], P('mp', 'dp'), may hold values from -0.375 to 0.375
- second_factor: bfloat16 [32, 256, 256], P('mp', 'dp'), may hold values from -0.375 to 0.375
Outputs:
- mixed: bfloat16 [32768, 8192], P('dp', 'mp')
- grad_tokens: bfloat16 [32768, 8192], P('dp', 'mp')
- grad_first: float32 [32, 256, 256], P('mp', 'dp')
- grad_second: float32 [32, 256, 256], P('mp', 'dp')
All inputs are finite; a program needn't handle non-finite values.
Results may differ from a plain program's by a relative error of at most 0.0056.
Values may be sent and summed in bfloat16 or wider, within the bound.
A program may use at most 64 MiB of HBM per device.

v0:
```python
import math

import jax
import jax.numpy as jnp
from jax import lax
from jax.sharding import PartitionSpec as P

BLOCKS = 32
BLK = 256


def gelu_exact(value):
    return jax.nn.gelu(value, approximate=False)


def add_rows(acts, shard_rows):
    return jnp.einsum("tbi,bio->tbo", acts, shard_rows, preferred_element_type=jnp.float32)


def on_device(tokens, upstream, first_factor, second_factor):
    tok_count = tokens.shape[0]
    local_blocks = first_factor.shape[0]
    group_count = lax.axis_size("mp")
    slice_width = BLK // group_count
    inner_span = BLK // BLOCKS
    scale = 1.0 / math.sqrt(tok_count * lax.axis_size("dp"))
    acts = tokens.reshape(tok_count, local_blocks, BLK)
    first_out = add_rows(acts, lax.all_gather(first_factor, "dp", axis=1, tiled=True))
    first_out = first_out.astype(jnp.bfloat16)
    outgoing = jnp.transpose(
        first_out.reshape(tok_count, local_blocks, group_count, slice_width), (2, 0, 1, 3)
    )
    outgoing = outgoing.reshape(group_count, tok_count, local_blocks * slice_width)
    incoming = lax.all_to_all(outgoing, "mp", split_axis=0, concat_axis=0, tiled=True)
    moved_in = incoming.reshape(group_count, tok_count, local_blocks, local_blocks, inner_span)
    moved_in = jnp.transpose(moved_in, (1, 3, 4, 0, 2)).reshape(tok_count, local_blocks, BLK)
    second_out = add_rows(moved_in, lax.all_gather(second_factor, "dp", axis=1, tiled=True))
    activated, pullback = jax.vjp(gelu_exact, second_out)
    mixed = (tokens.astype(jnp.float32) + activated.reshape(tok_count, local_blocks * BLK)).astype(
        jnp.bfloat16
    )
    upstream_rows = upstream.astype(jnp.float32)
    grad_out = pullback(upstream_rows.reshape(tok_count, local_blocks, BLK))[0].astype(jnp.bfloat16)
    right_term = jnp.einsum("tjc,tjk->jck", moved_in, grad_out, preferred_element_type=jnp.float32)
    grad_second = lax.psum_scatter(right_term, "dp", scatter_dimension=1, tiled=True) * scale
    grad_moved = jnp.einsum(
        "tjk,jck->tjc",
        grad_out,
        lax.all_gather(second_factor, "dp", axis=1, tiled=True),
        preferred_element_type=jnp.float32,
    )
    grad_moved = grad_moved.astype(jnp.bfloat16)
    returning = grad_moved.reshape(tok_count, local_blocks, inner_span, group_count, local_blocks)
    returning = jnp.transpose(returning, (3, 0, 4, 1, 2)).reshape(
        group_count, tok_count, local_blocks * slice_width
    )
    arrived = lax.all_to_all(returning, "mp", split_axis=0, concat_axis=0, tiled=True)
    grad_inner = jnp.transpose(
        arrived.reshape(group_count, tok_count, local_blocks, slice_width), (1, 2, 0, 3)
    )
    grad_inner = grad_inner.reshape(tok_count, local_blocks, BLK)
    left_term = jnp.einsum("tbi,tbo->bio", acts, grad_inner, preferred_element_type=jnp.float32)
    grad_first = lax.psum_scatter(left_term, "dp", scatter_dimension=1, tiled=True) * scale
    back_proj = jnp.einsum(
        "tbo,bio->tbi",
        grad_inner,
        lax.all_gather(first_factor, "dp", axis=1, tiled=True),
        preferred_element_type=jnp.float32,
    )
    grad_tokens = (upstream_rows + back_proj.reshape(tok_count, local_blocks * BLK)).astype(
        jnp.bfloat16
    )
    return (mixed, grad_tokens, grad_first, grad_second)


def solution(mesh):
    placed = (P("dp", "mp"), P("dp", "mp"), P("mp", "dp", None), P("mp", "dp", None))
    return jax.shard_map(
        on_device,
        mesh=mesh,
        in_specs=placed,
        out_specs=(P("dp", "mp"), P("dp", "mp"), P("mp", "dp", None), P("mp", "dp", None)),
        check_vma=False,
    )
```

profile of v0, /device:TPU:6, one launch (start us, length us, event | category | flops | bytes accessed | tf_op | source)
XLA Modules:
  0.0 1371.5 jit_solution(15681795561861110920)
XLA Ops:
  7.2 0.7 copy.37
  7.9 214.0 %all_gather.8 = bf16[4,256,256]{2,0,1:T(4,128)(2,1)S(1)} all-gather(bf16[4,4,256]{2,0,1:T(4,128)(2,1)S(1)} %copy.37), channel_id=1, replica_groups=mesh['dp'=64,'mp'=8] {'dp'}, dimensions={1}, use_global_device_ids=true | all-gather | bytes 532480 | tf_op jit(solution)/shard_map/all_gather | solution.py:28
  221.9 1.7 convolution_convert_fusion.1
  223.7 1.0 copy.40
  224.7 3.6 all-to-all-start
  228.3 1.6 copy.46
  229.9 229.3 %all_gather.9 = bf16[4,256,256]{2,0,1:T(4,128)(2,1)S(1)} all-gather(bf16[4,4,256]{2,0,1:T(4,128)(2,1)S(1)} %copy.42), channel_id=1, replica_groups=mesh['dp'=64,'mp'=8] {'dp'}, dimensions={1}, use_global_device_ids=true | all-gather | bytes 532480 | tf_op jit(solution)/shard_map/all_gather | solution.py:37
  459.3 0.5 copy.41
  459.8 1.0 copy-done.3
  460.9 6.7 fusion.7
  467.6 1.4 fusion.20
  469.0 2.1 reshape.51
  471.1 2.8 copy.49
  473.9 4.7 all-to-all-start.1
  478.6 0.0 all-reduce.5.cloned.1.call-start
  478.6 0.5 fusion.27
  479.1 1.7 copy.58
  480.8 24.4 %all-to-all-done.1 = bf16[8,512,128]{1,2,0:T(8,128)(2,1)} async-done(((bf16[8,512,128]{1,2,0:T(8,128)(2,1)}), bf16[8,512,128]{1,2,0:T(8,128)(2,1)}, u32[]{:S(2)}, u32[]{:S(2)}) %all-to-all-start.1) | async-done | bytes 1048608 | tf_op jit(solution)/shard_map/all_to_all | solution.py:57
  505.2 1.3 copy.50
  506.5 1.4 convolution_bitcast_fusion
  507.9 2.5 copy.55
  510.5 0.0 all-reduce.5.cloned.1.call-update
  510.5 1.3 dynamic-slice
  512.4 4.1 bitcast_multiply_fusion.3
  516.5 2.9 copy.45
  519.4 1.8 fusion.31
  521.2 3.0 copy.53
  524.2 3.9 add_convert_fusion
  528.1 834.6 %all-reduce.5.cloned.1.call-done = (f32[4,256,256]{2,0,1:T(4,128)}, f32[4,256,256]{2,0,1:T(4,128)}) async-done(((f32[4,256,256]{2,0,1:T(4,128)}, f32[4,256,256]{2,0,1:T(4,128)}), (f32[4,256,256]{2,0,1:T(4,128)}, f32[4,256,256]{2,0,1:T(4,128)})) %all-reduce.5.cloned.1.call-update) | async-done | bytes 2097168
  1362.7 0.7 dynamic-slice_multiply_fusion
  1363.5 0.6 copy.60
  1364.1 0.6 copy.59
  (11 shorter events, 0.0 us)
Async XLA Ops:
  223.6 4.6 copy-start.4
  223.6 4.6 copy-start.2
  224.7 234.6 %all-to-all-start = ((bf16[8,512,128]{1,2,0:T(8,128)(2,1)}), bf16[8,512,128]{1,2,0:T(8,128)(2,1)S(1)}, u32[]{:S(2)}, u32[]{:S(2)}) async-start(bf16[8,512,128]{1,2,0:T(8,128)(2,1)} %bitcast.3), calls=%async_computation | async-start | bytes 2097152 | tf_op jit(solution)/shard_map/all_to_all | solution.py:34
  459.3 1.6 copy-start.3
  473.9 31.3 %all-to-all-start.1 = ((bf16[8,512,128]{1,2,0:T(8,128)(2,1)}), bf16[8,512,128]{1,2,0:T(8,128)(2,1)}, u32[]{:S(2)}, u32[]{:S(2)}) async-start(bf16[8,512,128]{1,2,0:T(8,128)(2,1)} %bitcast.119), calls=%async_computation.1 | async-start | bytes 2097152 | tf_op jit(solution)/shard_map/all_to_all | solution.py:57
  478.6 884.2 %all-reduce.5.cloned.1.call-start = ((), (), s32[]{:S(2)}) async-start(), calls=%async_computation.2 | async-start | bytes 4194304
  479.1 27.4 %copy-start = (bf16[512,1024]{1,0:T(8,128)(2,1)S(1)}, bf16[512,1024]{1,0:T(8,128)(2,1)}, u32[]{:S(2)}) copy-start(bf16[512,1024]{1,0:T(8,128)(2,1)} %param.4) | copy-start | bytes 3145732
  521.2 3.1 copy-start.1
Sparse Core Ops, SparseCore 0:
  510.6 852.0 all-reduce.4
where the time goes:
time: 1380 us; the launch traced here: 1370 us
  waiting for transfers between devices  859 us (62%)
  blocking collectives  443 us (32%)
  local copies, waits for them, and re-layouts  23.9 us (2%)
  between operations  14.8 us (1%)
    unnamed x2, waiting for transfers between devices  835 us
    all_gather x1, blocking collectives, on_device(): lax.all_gather(second_factor, 'dp', axis=1, tiled=True)  229 us
    all_gather x1, blocking collectives, on_device(): lax.all_gather(first_factor, 'dp', axis=1, tiled=True)  214 us
  transfers between devices with their start and end apart: 3, of which 2 were waited for; matrix products, arithmetic and copies ran while one was open for 2% of the time, Pallas kernels for 0%

commit v1 on v0

v1 whole, which is shorter than its diff:
```python
import functools
import math

import jax
import jax.numpy as jnp
from jax import lax
from jax.experimental import pallas as pl
from jax.experimental.pallas import tpu as pltpu
from jax.sharding import PartitionSpec as P

BLOCKS = 32
BLK = 256
NZ, NH, NX = 8, 2, 4
MESH = pl.DeviceIdType.MESH


def place():
    me = lax.axis_index("dp")
    return me // (NH * NX), (me // NX) % NH, me % NX


def dp_of(z, h, x):
    return (z * NH + h) * NX + x


def x_peers(x):
    return x + 1 - 2 * (x % 2), NX - 1 - x, (x + 2) % NX


def greet(z, h, x):
    near, far, _ = x_peers(x)
    peers = [dp_of(z, 1 - h, x), dp_of(z, h, near), dp_of(z, h, far)]
    peers += [dp_of((z + k) % NZ, h, x) for k in range(1, NZ)]
    barrier = pltpu.get_barrier_semaphore()
    for peer in peers:
        pl.semaphore_signal(barrier, inc=1, device_id={"dp": peer}, device_id_type=MESH)
    pl.semaphore_wait(barrier, len(peers))


def push(src, dst, sems, k, peer):
    return pltpu.make_async_remote_copy(
        src_ref=src, dst_ref=dst, send_sem=sems.at[0, k], recv_sem=sems.at[1, k],
        device_id={"dp": peer}, device_id_type=MESH,
    )


def gather_kernel(s_ref, o_ref, buf, sems, lsem):
    z, h, x = place()
    near, far, opp = x_peers(x)
    own = pltpu.make_async_copy(s_ref, buf.at[x, z, h], lsem.at[0])
    own.start()
    greet(z, h, x)
    step_y = push(s_ref, buf.at[x, z, h], sems, 0, dp_of(z, 1 - h, x))
    step_y.start()
    own.wait()
    step_y.wait()
    steps = []
    for k in range(1, NZ):
        c = push(buf.at[x, z], buf.at[x, z], sems, k, dp_of((z + k) % NZ, h, x))
        c.start()
        steps.append(c)
    for c in steps:
        c.wait()
    lo, hi = pl.ds(0, NZ // 2), pl.ds(NZ // 2, NZ // 2)
    to_near, to_far = dp_of(z, h, near), dp_of(z, h, far)
    n_lo = push(buf.at[x, lo], buf.at[x, lo], sems, 8, to_near)
    n_hi = push(buf.at[x, hi], buf.at[x, hi], sems, 9, to_near)
    f_hi = push(buf.at[x, hi], buf.at[x, hi], sems, 10, to_far)
    f_lo = push(buf.at[x, lo], buf.at[x, lo], sems, 11, to_far)
    n_lo.start()
    f_hi.start()
    n_hi.start()
    f_lo.start()
    n_lo.wait_recv()
    r_lo = push(buf.at[near, lo], buf.at[near, lo], sems, 12, to_far)
    r_lo.start()
    f_hi.wait_recv()
    r_hi = push(buf.at[far, hi], buf.at[far, hi], sems, 13, to_near)
    r_hi.start()
    n_hi.wait_recv()
    f_lo.wait_recv()
    r_lo.wait_recv()
    r_hi.wait_recv()
    for c in (n_lo, n_hi, f_hi, f_lo, r_lo, r_hi):
        c.wait_send()
    out = pltpu.make_async_copy(buf, o_ref, lsem.at[1])
    out.start()
    out.wait()


def gather(shard):
    rows = shard.shape[0]
    return pl.pallas_call(
        gather_kernel,
        out_shape=jax.ShapeDtypeStruct((NX, NZ, NH, rows, BLK), shard.dtype),
        in_specs=[pl.BlockSpec(memory_space=pltpu.VMEM)],
        out_specs=pl.BlockSpec(memory_space=pl.ANY),
        scratch_shapes=[
            pltpu.VMEM((NX, NZ, NH, rows, BLK), shard.dtype),
            pltpu.SemaphoreType.DMA((2, 14)),
            pltpu.SemaphoreType.DMA((2,)),
        ],
        compiler_params=pltpu.CompilerParams(collective_id=0, has_side_effects=True),
        name="gather_rows",
    )(shard)


def scatter_kernel(scale, g_ref, o_ref, s1, r1, s2, r2, s3, r3, t, s4, r4, sems):
    z, h, x = place()
    near, far, opp = x_peers(x)
    half = NZ // 2
    for k in range(2):
        zs = pl.ds(k * half, half)
        first = near if k == 0 else far
        s1[k, 0] = g_ref[first, zs].astype(jnp.bfloat16)
        s1[k, 1] = g_ref[opp, zs].astype(jnp.bfloat16)
    greet(z, h, x)
    peer = (dp_of(z, h, near), dp_of(z, h, far))
    ones = []
    for k in range(2):
        c = push(s1.at[k], r1.at[k], sems, k, peer[k])
        c.start()
        ones.append(c)
    twos = []
    for k in range(2):
        ones[k].wait_recv()
        zs = pl.ds(k * half, half)
        second = far if k == 0 else near
        s2[k] = (g_ref[second, zs] + r1[k, 1].astype(jnp.float32)).astype(jnp.bfloat16)
        c = push(s2.at[k], r2.at[k], sems, 2 + k, peer[1 - k])
        c.start()
        twos.append(c)
    for k in range(2):
        twos[k].wait_recv()
        zs = pl.ds(k * half, half)
        t[zs] = g_ref[x, zs] + r1[k, 0].astype(jnp.float32) + r2[k].astype(jnp.float32)
    s3[...] = t[...].astype(jnp.bfloat16)
    threes = []
    for k in range(1, NZ):
        to = (z + k) % NZ
        c = push(s3.at[to], r3.at[k - 1], sems, 3 + k, dp_of(to, h, x))
        c.start()
        threes.append(c)
    total = t[z]
    for k in range(1, NZ):
        threes[k - 1].wait_recv()
        total = total + r3[k - 1].astype(jnp.float32)
    t[0] = total
    s4[...] = t[0, 1 - h]
    last = push(s4, r4, sems, 11, dp_of(z, 1 - h, x))
    last.start()
    last.wait_recv()
    o_ref[...] = (t[0, h] + r4[...]) * scale
    for c in ones + twos + threes + [last]:
        c.wait_send()


def scatter(terms, scale):
    rows = terms.shape[3]
    half = NZ // 2
    tail = (NH, rows, BLK)
    bf, f32 = jnp.bfloat16, jnp.float32
    return pl.pallas_call(
        functools.partial(scatter_kernel, scale),
        out_shape=jax.ShapeDtypeStruct((rows, BLK), f32),
        in_specs=[pl.BlockSpec(memory_space=pltpu.VMEM)],
        out_specs=pl.BlockSpec(memory_space=pltpu.VMEM),
        scratch_shapes=[
            pltpu.VMEM((2, 2, half) + tail, bf),
            pltpu.VMEM((2, 2, half) + tail, bf),
            pltpu.VMEM((2, half) + tail, bf),
            pltpu.VMEM((2, half) + tail, bf),
            pltpu.VMEM((NZ,) + tail, bf),
            pltpu.VMEM((NZ - 1,) + tail, bf),
            pltpu.VMEM((NZ,) + tail, f32),
            pltpu.VMEM((rows, BLK), f32),
            pltpu.VMEM((rows, BLK), f32),
            pltpu.SemaphoreType.DMA((2, 12)),
        ],
        compiler_params=pltpu.CompilerParams(collective_id=1, has_side_effects=True),
        name="scatter_sums",
    )(terms)


def gelu_exact(value):
    return jax.nn.gelu(value, approximate=False)


def add_rows(acts, shard_rows):
    return jnp.einsum("tbi,bio->tbo", acts, shard_rows, preferred_element_type=jnp.float32)


def on_device(tokens, upstream, first_factor, second_factor):
    tok_count = tokens.shape[0]
    local_blocks = first_factor.shape[0]
    own_rows = first_factor.shape[1]
    group_count = lax.axis_size("mp")
    slice_width = BLK // group_count
    inner_span = BLK // BLOCKS
    scale = 1.0 / math.sqrt(tok_count * lax.axis_size("dp"))
    shard = jnp.stack([first_factor, second_factor]).reshape(2 * local_blocks * own_rows, BLK)
    rows = gather(shard).reshape(NX, NZ, NH, 2, local_blocks, own_rows, BLK)
    rows = jnp.transpose(rows, (3, 4, 1, 2, 0, 5, 6)).reshape(2, local_blocks, BLK, BLK)
    first_rows, second_rows = rows[0], rows[1]
    acts = tokens.reshape(tok_count, local_blocks, BLK)
    first_out = add_rows(acts, first_rows).astype(jnp.bfloat16)
    outgoing = jnp.transpose(
        first_out.reshape(tok_count, local_blocks, group_count, slice_width), (2, 0, 1, 3)
    )
    outgoing = outgoing.reshape(group_count, tok_count, local_blocks * slice_width)
    incoming = lax.all_to_all(outgoing, "mp", split_axis=0, concat_axis=0, tiled=True)
    moved_in = incoming.reshape(group_count, tok_count, local_blocks, local_blocks, inner_span)
    moved_in = jnp.transpose(moved_in, (1, 3, 4, 0, 2)).reshape(tok_count, local_blocks, BLK)
    second_out = add_rows(moved_in, second_rows)
    activated, pullback = jax.vjp(gelu_exact, second_out)
    mixed = (tokens.astype(jnp.float32) + activated.reshape(tok_count, local_blocks * BLK)).astype(
        jnp.bfloat16
    )
    upstream_rows = upstream.astype(jnp.float32)
    grad_out = pullback(upstream_rows.reshape(tok_count, local_blocks, BLK))[0].astype(jnp.bfloat16)
    right_term = jnp.einsum("tjc,tjk->jck", moved_in, grad_out, preferred_element_type=jnp.float32)
    grad_moved = jnp.einsum(
        "tjk,jck->tjc", grad_out, second_rows, preferred_element_type=jnp.float32
    )
    grad_moved = grad_moved.astype(jnp.bfloat16)
    returning = grad_moved.reshape(tok_count, local_blocks, inner_span, group_count, local_blocks)
    returning = jnp.transpose(returning, (3, 0, 4, 1, 2)).reshape(
        group_count, tok_count, local_blocks * slice_width
    )
    arrived = lax.all_to_all(returning, "mp", split_axis=0, concat_axis=0, tiled=True)
    grad_inner = jnp.transpose(
        arrived.reshape(group_count, tok_count, local_blocks, slice_width), (1, 2, 0, 3)
    )
    grad_inner = grad_inner.reshape(tok_count, local_blocks, BLK)
    left_term = jnp.einsum("tbi,tbo->bio", acts, grad_inner, preferred_element_type=jnp.float32)
    terms = jnp.stack([left_term, right_term])
    terms = terms.reshape(2, local_blocks, NZ, NH, NX, own_rows, BLK)
    terms = jnp.transpose(terms, (4, 2, 3, 0, 1, 5, 6))
    terms = terms.reshape(NX, NZ, NH, 2 * local_blocks * own_rows, BLK)
    sums = scatter(terms, scale).reshape(2, local_blocks, own_rows, BLK)
    back_proj = jnp.einsum(
        "tbo,bio->tbi", grad_inner, first_rows, preferred_element_type=jnp.float32
    )
    grad_tokens = (upstream_rows + back_proj.reshape(tok_count, local_blocks * BLK)).astype(
        jnp.bfloat16
    )
    return (mixed, grad_tokens, sums[0], sums[1])


def solution(mesh):
    placed = (P("dp", "mp"), P("dp", "mp"), P("mp", "dp", None), P("mp", "dp", None))
    return jax.shard_map(
        on_device,
        mesh=mesh,
        in_specs=placed,
        out_specs=placed,
        check_vma=False,
    )
```

time: 1380 us -> 172 us (0.12)
  waiting for transfers between devices: 859 us -> 42.8 us
  blocking collectives: 443 us -> 0 us
  Pallas kernels: 0 us -> 66.6 us
  between operations: 14.8 us -> 0.77 us
    unnamed x2 -> x0, waiting for transfers between devices: 835 us -> none
    all_gather x2 -> x0, blocking collectives: 443 us -> none  [the longest x1 229 us: on_device(): lax.all_gather(second_factor, 'dp', axis=1, tiled=True)]
    pallas_call x0 -> x2, Pallas kernels: none -> 66.6 us  [the longest x1 35.5 us: gather(): pl.pallas_call(gather_kernel, out_shape=jax.ShapeDtypeStruct((NX, NZ, NH,...]
    all_to_all x1, waiting for transfers between devices: 0.01 us -> 24.8 us  [on_device(): lax.all_to_all(outgoing, 'mp', split_axis=0, concat_axis=0, tiled=True)]
  transfers between devices with their start and end apart: 3 -> 2, of which waited for: 2 -> 2; matrix products, arithmetic and copies ran while one was open for 2% -> 6% of each run, Pallas kernels for 0% -> 0%
where the time goes in v1:
time: 172 us; the launch traced here: 171 us
  Pallas kernels  66.6 us (39%)
  waiting for transfers between devices  42.8 us (25%)
  local copies, waits for them, and re-layouts  28.1 us (16%)
  matrix products  13.2 us (8%)
  other arithmetic  11.6 us (7%)
  starting transfers between devices  7.82 us (5%)
    pallas_call x1, Pallas kernels, gather(): pl.pallas_call(gather_kernel, out_shape=jax.ShapeDtypeStruct((NX, NZ, NH,...  35.5 us
    pallas_call x1, Pallas kernels, scatter(): pl.pallas_call(functools.partial(scatter_kernel, scale), out_shape=jax.Sh...  31.1 us
    all_to_all x1, waiting for transfers between devices, on_device(): lax.all_to_all(outgoing, 'mp', split_axis=0, concat_axis=0, tiled=True)  24.8 us
    all_to_all x1, waiting for transfers between devices, on_device(): lax.all_to_all(returning, 'mp', split_axis=0, concat_axis=0, tiled=True)  18 us
    dot_general x2, matrix products, add_rows(): jnp.einsum('tbi,bio->tbo', acts, shard_rows, preferred_element_type=jnp.f...  8.43 us
    reshape x2, local copies, waits for them, and re-layouts, on_device(): grad_moved.reshape(tok_count, local_blocks, inner_span, group_count, loca...  4.91 us
    convert_element_type x1, other arithmetic, on_device(): (upstream_rows + back_proj.reshape(tok_count, local_blocks * BLK)).astype...  4.58 us
    all_to_all x1, starting transfers between devices, on_device(): lax.all_to_all(returning, 'mp', split_axis=0, concat_axis=0, tiled=True)  4.26 us
  transfers between devices with their start and end apart: 2, of which 2 were waited for; matrix products, arithmetic and copies ran while one was open for 6% of the time, Pallas kernels for 0%

profile of v1, /device:TPU:6, one launch (start us, length us, event | category | flops | bytes accessed | tf_op | source)
XLA Modules:
  0.0 170.8 jit_solution(5364811025515785741)
XLA Ops:
  0.6 0.7 pad_maximum_fusion.1
  1.4 0.6 reshape.68.s_ref
  2.0 35.5 %gather_rows.1 = bf16[4,8,2,32,256]{4,3,2,1,0:T(8,128)(2,1)} custom-call(bf16[32,256]{1,0:T(8,128)(2,1)} %reshape.68.s_ref), custom_call_target="tpu_custom_call" | custom-call | tf_op jit(solution)/shard_map/gather_rows/pallas_call | solution.py:93
  37.5 1.3 reshape.69
  39.4 1.3 fusion.31
  41.8 1.0 copy.25
  42.9 3.6 %all-to-all-start = ((bf16[8,512,128]{1,2,0:T(8,128)(2,1)}), bf16[8,512,128]{1,2,0:T(8,128)(2,1)S(1)}, u32[]{:S(2)}, u32[]{:S(2)}) async-start(bf16[8,512,128]{1,2,0:T(8,128)(2,1)} %bitcast.8), calls=%async_computation | async-start | bytes 2097152 | tf_op jit(solution)/shard_map/all_to_all | solution.py:211
  46.4 1.6 copy.30
  48.1 24.8 %all-to-all-done = bf16[8,512,128]{1,2,0:T(8,128)(2,1)S(1)} async-done(((bf16[8,512,128]{1,2,0:T(8,128)(2,1)}), bf16[8,512,128]{1,2,0:T(8,128)(2,1)S(1)}, u32[]{:S(2)}, u32[]{:S(2)}) %all-to-all-start) | async-done | bytes 1048608 | tf_op jit(solution)/shard_map/all_to_all | solution.py:211
  73.5 1.0 copy-done.6
  74.5 7.9 %fusion.7 = (bf16[512,4,256]{0,2,1:T(8,128)(2,1)S(1)}, f32[512,4,256]{0,2,1:T(8,128)}, f32[4,256,512]{2,1,0:T(8,128)}) fusion(f32[512,4,256]{0,2,1:T(8,128)S(1)} %bitcast.131, bf16[512,4,256]{0,1,2:T(4,128)(2,1)S(1)} %bitcast.125, bf16[4,256,256]{2,0,1:T(4,128)(2,1)} %bitcast.132), kind=kOutput, calls=%fused_computation.16 | convolution fusion | flops 306184192 | bytes 8912896 | tf_op jit(solution)/shard_map/tbi,bio->tbo/dot_general | solution.py:190
  82.5 1.4 fusion.20
  83.9 2.1 %reshape.77 = bf16[512,4,8,8,4]{0,4,3,2,1:T(4,128)(2,1)} reshape(bf16[512,4,256]{0,2,1:T(8,128)(2,1)} %fusion.20) | data formatting | bytes 2097152 | tf_op jit(solution)/shard_map/reshape | solution.py:226
  86.0 2.8 %copy.33 = bf16[512,4,8,8,4]{0,2,1,4,3:T(8,128)(2,1)} copy(bf16[512,4,8,8,4]{0,4,3,2,1:T(4,128)(2,1)} %reshape.77) | data formatting | bytes 2097152 | tf_op jit(solution)/shard_map/reshape | solution.py:226
  88.8 4.3 %all-to-all-start.1 = ((bf16[8,512,128]{1,2,0:T(8,128)(2,1)}), bf16[8,512,128]{1,2,0:T(8,128)(2,1)}, u32[]{:S(2)}, u32[]{:S(2)}) async-start(bf16[8,512,128]{1,2,0:T(8,128)(2,1)} %bitcast.127), calls=%async_computation.1 | async-start | bytes 2097152 | tf_op jit(solution)/shard_map/all_to_all | solution.py:230
  93.0 1.5 fusion.23
  94.5 2.5 %stack.22 = f32[1,4,8,2,4,4,256]{6,5,4,3,2,1,0:T(4,128)} reshape(f32[4,256,256]{2,1,0:T(8,128)} %fusion.23) | data formatting | bytes 2097152 | tf_op jit(solution)/shard_map/stack | solution.py:236
  97.0 2.8 %bitcast_multiply_fusion.3 = f32[512,4,256]{0,2,1:T(8,128)S(1)} fusion(f32[512,4,256]{0,2,1:T(8,128)} %get-tuple-element.5, f32[4,256,512]{2,1,0:T(8,128)} %get-tuple-element.10), kind=kLoop, calls=%fused_computation.10 | loop fusion | flops 1048576 | bytes 6291456 | tf_op jit(solution)/shard_map/jvp()/mul | solution.py:186
  99.8 1.8 %copy.29 = f32[512,1024]{1,0:T(8,128)} copy(f32[512,1024]{0,1:T(8,128)S(1)} %bitcast.121) | data formatting | bytes 4194304 | tf_op jit(solution)/shard_map/reshape | solution.py:216
  101.6 18.0 %all-to-all-done.1 = bf16[8,512,128]{1,2,0:T(8,128)(2,1)} async-done(((bf16[8,512,128]{1,2,0:T(8,128)(2,1)}), bf16[8,512,128]{1,2,0:T(8,128)(2,1)}, u32[]{:S(2)}, u32[]{:S(2)}) %all-to-all-start.1) | async-done | bytes 1048608 | tf_op jit(solution)/shard_map/all_to_all | solution.py:230
  119.6 1.3 copy.34
  120.9 1.4 convolution_bitcast_fusion
  122.8 0.8 copy-done.2
  123.6 1.3 stack.21
  124.9 3.5 %copy_bitcast_fusion = f32[4,8,2,2,4,4,256]{6,5,4,3,2,1,0:T(4,128)} fusion(f32[1,4,8,2,4,4,256]{6,5,4,3,2,1,0:T(4,128)} %stack.22, f32[1,4,8,2,4,4,256]{6,5,4,3,2,1,0:T(4,128)} %stack.21), kind=kLoop, calls=%fused_computation.3 | loop fusion | flops 524288 | bytes 4194304 | tf_op jit(solution)/shard_map/transpose | solution.py:238
  128.3 3.0 %reshape.82.g_ref = f32[4,8,2,32,256]{4,3,2,1,0:T(8,128)} reshape(f32[4,8,2,2,4,4,256]{6,5,4,3,2,1,0:T(4,128)} %copy_bitcast_fusion) | data formatting | bytes 4194304 | tf_op jit(solution)/shard_map/reshape | solution.py:239
  131.3 31.1 %scatter_sums.1 = f32[32,256]{1,0:T(8,128)} custom-call(f32[4,8,2,32,256]{4,3,2,1,0:T(8,128)} %reshape.82.g_ref), custom_call_target="tpu_custom_call" | custom-call | tf_op jit(solution)/shard_map/scatter_sums/pallas_call | solution.py:163
  162.4 0.7 fusion.32
  163.2 0.6 squeeze.15
  163.8 0.6 squeeze.14
  164.4 1.8 %copy.37 = f32[512,1024]{1,0:T(8,128)} copy(f32[512,1024]{0,1:T(8,128)S(1)} %bitcast.122) | data formatting | bytes 4194304 | tf_op jit(solution)/shard_map/reshape | solution.py:244
  166.3 4.6 %add_convert_fusion = (bf16[512,1024]{1,0:T(8,128)(2,1)}, bf16[512,1024]{1,0:T(8,128)(2,1)}) fusion(f32[512,1024]{1,0:T(8,128)} %copy.37, bf16[512,1024]{1,0:T(8,128)(2,1)S(1)} %copy-done.4, f32[512,1024]{1,0:T(8,128)} %copy.29, bf16[512,1024]{1,0:T(8,128)(2,1)} %param.4), kind=kLoop, calls=%fused_computation.17 | loop fusion | flops 3145728 | bytes 8388608 | tf_op jit(solution)/shard_map/convert_element_type | solution.py:244
  (19 shorter events, 2.6 us)
Async XLA Ops:
  38.8 1.9 %copy-start.5 = (bf16[512,1024]{1,0:T(8,128)(2,1)S(1)}, bf16[512,1024]{1,0:T(8,128)(2,1)}, u32[]{:S(2)}) copy-start(bf16[512,1024]{1,0:T(8,128)(2,1)} %param.4) | copy-start | bytes 3145732
  40.8 1.0 copy-start
  41.8 4.6 %copy-start.3 = (bf16[512,1024]{1,0:T(8,128)(2,1)S(1)}, bf16[512,1024]{1,0:T(8,128)(2,1)}, u32[]{:S(2)}) copy-start(bf16[512,1024]{1,0:T(8,128)(2,1)} %param.5) | copy-start | bytes 3145732
  42.9 30.1 %all-to-all-start = ((bf16[8,512,128]{1,2,0:T(8,128)(2,1)}), bf16[8,512,128]{1,2,0:T(8,128)(2,1)S(1)}, u32[]{:S(2)}, u32[]{:S(2)}) async-start(bf16[8,512,128]{1,2,0:T(8,128)(2,1)} %bitcast.8), calls=%async_computation | async-start | bytes 2097152 | tf_op jit(solution)/shard_map/all_to_all | solution.py:211
  72.9 1.6 copy-start.6
  74.5 7.9 %copy-start.7 = (bf16[1,4,8,2,4,4,256]{6,1,5,4,3,2,0:T(4,128)(2,1)S(1)}, bf16[1,4,8,2,4,4,256]{6,1,5,4,3,2,0:T(4,128)(2,1)}, u32[]{:S(2)}) copy-start(bf16[1,4,8,2,4,4,256]{6,1,5,4,3,2,0:T(4,128)(2,1)} %get-tuple-element.6) | copy-start | bytes 1572868
  88.8 30.8 %all-to-all-start.1 = ((bf16[8,512,128]{1,2,0:T(8,128)(2,1)}), bf16[8,512,128]{1,2,0:T(8,128)(2,1)}, u32[]{:S(2)}, u32[]{:S(2)}) async-start(bf16[8,512,128]{1,2,0:T(8,128)(2,1)} %bitcast.127), calls=%async_computation.1 | async-start | bytes 2097152 | tf_op jit(solution)/shard_map/all_to_all | solution.py:230
  120.9 1.5 copy-start.1
  122.4 1.2 copy-start.2
  164.4 1.8 %copy-start.4 = (bf16[512,1024]{1,0:T(8,128)(2,1)S(1)}, bf16[512,1024]{1,0:T(8,128)(2,1)}, u32[]{:S(2)}) copy-start(bf16[512,1024]{1,0:T(8,128)(2,1)} %param.5) | copy-start | bytes 3145732

commit v2 on v0

v2 whole, which is shorter than its diff:
```python
import functools
import math

import jax
import jax.numpy as jnp
from jax import lax
from jax.experimental import pallas as pl
from jax.experimental.pallas import tpu as pltpu
from jax.sharding import PartitionSpec as P

BLK = 256
LOC = 4
ROWS = 4
NZ, NH, NX = 8, 2, 4
NY, NC = 4, 2
NM = NY * NC
FEAT = LOC * BLK
CHUNKS = 4
HALF = NZ // 2
BF, F32 = jnp.bfloat16, jnp.float32
MESH = pl.DeviceIdType.MESH


def dp_of(z, h, x):
    return (z * NH + h) * NX + x


def nn(a, b):
    return lax.dot_general(a, b, (((1,), (0,)), ((), ())), preferred_element_type=F32)


def nt(a, b):
    return lax.dot_general(a, b, (((1,), (1,)), ((), ())), preferred_element_type=F32)


def tn(a, b):
    return lax.dot_general(a, b, (((0,), (0,)), ((), ())), preferred_element_type=F32)


def natural_of_send(s):
    return ((s >> 5) & 3) * 256 + (s >> 7) * 32 + (s & 31)


def arrived_of_sorted(v):
    j, x, oo, h, b = v >> 8, (v >> 6) & 3, (v >> 3) & 7, (v >> 2) & 1, v & 3
    return (h * 4 + x) * 128 + b * 32 + j * 8 + oo


def natural_of_gathered(p):
    return ((p >> 2) & 3) * 256 + ((p >> 4) & 15) * 16 + (p >> 8) * 4 + (p & 3)


def sorted_of_gathered(p):
    return ((p >> 2) & 3) * 256 + (p >> 8) * 64 + ((p >> 4) & 15) * 4 + (p & 3)


def natural_of_sorted(s):
    return ((s >> 2) & 15) * 16 + (s >> 6) * 4 + (s & 3)


def write_perm(ref, source_of):
    rows, cols = ref.shape
    source = source_of(lax.broadcasted_iota(jnp.int32, (1, cols), 1))

    @pl.loop(0, rows // 128)
    def _(k):
        at = pl.ds(pl.multiple_of(k * 128, 128), 128)
        row = lax.broadcasted_iota(jnp.int32, (128, cols), 0) + k * 128
        ref[at, :] = jnp.where(row == source, 1.0, 0.0).astype(BF)


def kernel(
    scale, x_ref, up_ref, shard_ref,
    mixed_ref, gtok_ref, gfac_ref,
    buf, w1, w2, xs, p_send, p_sort, p_nat, p_srt, p_x,
    u_tmp, send_a, recv_a, send_b, recv_b,
    g, s1, r1, s2, r2, t, s3, r3, s4, r4,
    gsem, lsem, sem_a, sem_b, rsem,
):
    me, mp = lax.axis_index("dp"), lax.axis_index("mp")
    z, h, x = me // (NH * NX), (me // NX) % NH, me % NX
    near, far, opp = x + 1 - 2 * (x % 2), NX - 1 - x, (x + 2) % NX
    yl, core = mp // NC, mp % NC
    ys = (yl, yl + 1 - 2 * (yl % 2), NY - 1 - yl, (yl + 2) % NY)
    mates = [ys[0] * NC + 1 - core]
    for k in (1, 2, 3):
        mates += [ys[k] * NC + core, ys[k] * NC + 1 - core]
    to_y, to_near, to_far = dp_of(z, 1 - h, x), dp_of(z, h, near), dp_of(z, h, far)
    to_z = [dp_of((z + k) % NZ, h, x) for k in range(1, NZ)]
    tc = x_ref.shape[0] // CHUNKS

    def push(src, dst, sems, k, peer):
        return pltpu.make_async_remote_copy(
            src_ref=src, dst_ref=dst, send_sem=sems.at[0, k], recv_sem=sems.at[1, k],
            device_id={"dp": peer}, device_id_type=MESH,
        )

    def swap(src, dst, sems, c, k):
        return pltpu.make_async_remote_copy(
            src_ref=src, dst_ref=dst, send_sem=sems.at[0, c, k], recv_sem=sems.at[1, c, k],
            device_id={"mp": mates[k]}, device_id_type=MESH,
        )

    def own(f):
        return pltpu.make_async_copy(shard_ref.at[f], buf.at[f, x, z, h], lsem.at[f])

    def gather_h(f):
        return push(shard_ref.at[f], buf.at[f, x, z, h], gsem.at[f], 0, to_y)

    def gather_z(f):
        part = buf.at[f, x, z]
        return [push(part, part, gsem.at[f], k, to_z[k - 1]) for k in range(1, NZ)]

    def gather_x(f):
        halves = [pl.ds(0, HALF), pl.ds(HALF, HALF)]

        def one(slot, half, k, peer):
            part = buf.at[f, slot, halves[half]]
            return push(part, part, gsem.at[f], k, peer)

        first = [one(x, 0, 8, to_near), one(x, 1, 9, to_far), one(x, 1, 10, to_near), one(x, 0, 11, to_far)]
        return first, lambda: [one(near, 0, 12, to_far), one(far, 1, 13, to_near)]

    def start(copies):
        for c in copies:
            c.start()

    def wait(copies):
        for c in copies:
            c.wait()

    for f in range(2):
        own(f).start()
    barrier = pltpu.get_barrier_semaphore()
    for peer in [to_y, to_near, to_far] + to_z:
        pl.semaphore_signal(barrier, inc=1, device_id={"dp": peer}, device_id_type=MESH)
    for mate in mates:
        pl.semaphore_signal(barrier, inc=1, device_id={"mp": mate}, device_id_type=MESH)
    pl.semaphore_wait(barrier, 3 + len(to_z) + len(mates))
    for f in range(2):
        gather_h(f).start()
    for f in range(2):
        own(f).wait()
    write_perm(p_x, natural_of_sorted)
    for f in range(2):
        gather_h(f).wait()
        start(gather_z(f))
    write_perm(p_nat, natural_of_gathered)
    write_perm(p_send, natural_of_send)
    wait(gather_z(0))
    first, relays = gather_x(0)
    relay = relays()
    start(first)
    write_perm(p_sort, arrived_of_sorted)
    for k in range(2):
        first[k].wait_recv()
        relay[k].start()
    write_perm(p_srt, sorted_of_gathered)
    g[...] = jnp.zeros_like(g)
    for k in range(2):
        first[2 + k].wait_recv()
        relay[k].wait_recv()
    for c in first + relay:
        c.wait_send()
    wait(gather_z(1))
    start(gather_x(1)[0])

    def sort_rows(f, perm, dest):
        rows = buf[f].reshape(FEAT, BLK)
        for b in range(LOC):
            dest[b] = nn(perm[b * BLK : (b + 1) * BLK, :], rows).astype(BF)

    sort_rows(0, p_nat, w1)

    def chunk(c):
        return pl.ds(pl.multiple_of(c * tc, tc), tc)

    def block(b):
        return slice(b * BLK, (b + 1) * BLK)

    def spread(values, send, recv, sems, c):
        for n in range(NM):
            send[c, n] = values(n)
        for k in range(NM - 1):
            swap(send.at[c, mates[k]], recv.at[c, mp], sems, c, k).start()
        recv[c, mp] = send[c, mp]

    def collect(recv, send, sems, c):
        for k in range(NM - 1):
            swap(send.at[c, mates[k]], recv.at[c, mates[k]], sems, c, k).wait_recv()
        return jnp.concatenate([recv[c, n] for n in range(NM)], axis=1)

    def permuted_send(perm_tile, send, recv, sems, c):
        done = {}

        def lanes(n):
            if n % 2 == 0:
                done[0] = perm_tile(n // 2).astype(BF)
            return done[0][:, (n % 2) * 128 : (n % 2 + 1) * 128]

        spread(lanes, send, recv, sems, c)

    @pl.loop(0, CHUNKS)
    def _(c):
        at = chunk(c)
        for b in range(LOC):
            u_tmp[:, block(b)] = nn(x_ref[at, block(b)], w1[b]).astype(BF)
        permuted_send(lambda k: nn(u_tmp[...], p_send[:, block(k)]), send_a, recv_a, sem_a, c)

        @pl.when(c == 1)
        def _():
            first, relays = gather_x(1)
            relay = relays()
            for k in range(2):
                first[k].wait_recv()
                relay[k].start()

        for b in range(LOC):
            xs[at, block(b)] = nn(x_ref[at, block(b)], p_x[...]).astype(BF)

    first, relays = gather_x(1)
    relay = relays()
    for k in range(2):
        first[2 + k].wait_recv()
        relay[k].wait_recv()
    for c in first + relay:
        c.wait_send()
    sort_rows(1, p_srt, w2)

    @pl.loop(0, CHUNKS)
    def _(c):
        at = chunk(c)
        arrived = collect(recv_a, send_a, sem_a, c)
        for j in range(LOC):
            v = nn(arrived, p_sort[:, block(j)]).astype(BF)
            y = nn(v, w2[j])
            cdf = 0.5 * (1.0 + lax.erf(y * math.sqrt(0.5)))
            mixed_ref[at, block(j)] = (x_ref[at, block(j)].astype(F32) + y * cdf).astype(BF)
            slope = cdf + y * (jnp.exp(-0.5 * y * y) * (1.0 / math.sqrt(2.0 * math.pi)))
            cot = (up_ref[at, block(j)].astype(F32) * slope).astype(BF)
            g[1, j] += tn(v, cot).reshape(NX, 2, 32, BLK)
            u_tmp[:, block(j)] = nt(cot, w2[j]).astype(BF)
        permuted_send(lambda k: nt(u_tmp[...], p_sort[block(k), :]), send_b, recv_b, sem_b, c)

    peer = (to_near, to_far)

    def sum_x1(f, k):
        return push(s1.at[f, k], r1.at[f, k], rsem.at[f], k, peer[k])

    def sum_x2(f, k):
        return push(s2.at[f, k], r2.at[f, k], rsem.at[f], 2 + k, peer[1 - k])

    def sum_z(f):
        return [push(s3.at[f, (z + k) % NZ], r3.at[f, k - 1], rsem.at[f], 3 + k, to_z[k - 1]) for k in range(1, NZ)]

    def sum_h(f):
        return push(s4.at[f], r4.at[f], rsem.at[f], 11, to_y)

    def reduce_x1(f):
        for k in range(2):
            s1[f, k, 0] = g[f, :, (near, far)[k], k].astype(BF)
            s1[f, k, 1] = g[f, :, opp, k].astype(BF)
            sum_x1(f, k).start()

    def reduce_x2(f):
        for k in range(2):
            sum_x1(f, k).wait_recv()
            s2[f, k] = (g[f, :, (far, near)[k], k] + r1[f, k, 1].astype(F32)).astype(BF)
            sum_x2(f, k).start()

    def reduce_z(f):
        for k in range(2):
            sum_x2(f, k).wait_recv()
            part = g[f, :, x, k] + r1[f, k, 0].astype(F32) + r2[f, k].astype(F32)
            t[f, :, k * HALF : (k + 1) * HALF] = part.reshape(LOC, HALF, NH * ROWS, BLK)
        for k in range(NZ):
            s3[f, k] = t[f, :, k].reshape(LOC * NH * ROWS, BLK).astype(BF)
        start(sum_z(f))

    def reduce_h(f):
        total = t[f, :, z].reshape(LOC * NH * ROWS, BLK)
        copies = sum_z(f)
        for k in range(NZ - 1):
            copies[k].wait_recv()
            total = total + r3[f, k].astype(F32)
        s4[f] = total
        sum_h(f).start()

    def reduce_end(f):
        sum_h(f).wait_recv()
        total = ((s4[f] + r4[f]) * scale).reshape(LOC, NH * ROWS, BLK)
        gfac_ref[f] = jnp.where(h == 0, total[:, :ROWS], total[:, ROWS:])
        for k in range(2):
            sum_x1(f, k).wait_send()
            sum_x2(f, k).wait_send()
        for c in sum_z(f):
            c.wait_send()
        sum_h(f).wait_send()

    reduce_x1(1)

    @pl.loop(0, CHUNKS)
    def _(c):
        at = chunk(c)
        arrived = collect(recv_b, send_b, sem_b, c)
        for b in range(LOC):
            du = nt(arrived, p_send[block(b), :]).astype(BF)
            g[0, b] += tn(xs[at, block(b)], du).reshape(NX, 2, 32, BLK)
            back = nt(du, w1[b])
            gtok_ref[at, block(b)] = (up_ref[at, block(b)].astype(F32) + back).astype(BF)
        for step, run in enumerate((reduce_x2, reduce_z, reduce_h)):
            pl.when(c == step)(functools.partial(run, 1))

    for run in (reduce_x1, reduce_x2, reduce_z, reduce_h):
        run(0)
    reduce_end(1)
    reduce_end(0)

    @pl.loop(0, CHUNKS)
    def _(c):
        for k in range(NM - 1):
            swap(send_a.at[c, mates[k]], recv_a.at[c, mp], sem_a, c, k).wait_send()
            swap(send_b.at[c, mates[k]], recv_b.at[c, mp], sem_b, c, k).wait_send()


def on_device(tokens, upstream, first_factor, second_factor):
    tok = tokens.shape[0]
    tc = tok // CHUNKS
    scale = 1.0 / math.sqrt(tok * lax.axis_size("dp"))
    shard = jnp.stack([first_factor, second_factor]).reshape(2, LOC * ROWS, BLK)
    vmem = pl.BlockSpec(memory_space=pltpu.VMEM)
    dma = pltpu.SemaphoreType.DMA
    slot = NH * ROWS
    mixed, gtok, gfac = pl.pallas_call(
        functools.partial(kernel, scale),
        out_shape=(
            jax.ShapeDtypeStruct((tok, FEAT), BF),
            jax.ShapeDtypeStruct((tok, FEAT), BF),
            jax.ShapeDtypeStruct((2, LOC, ROWS, BLK), F32),
        ),
        in_specs=[vmem, vmem, vmem],
        out_specs=(vmem, vmem, vmem),
        scratch_shapes=[
            pltpu.VMEM((2, NX, NZ, NH, LOC * ROWS, BLK), BF),
            pltpu.VMEM((LOC, BLK, BLK), BF),
            pltpu.VMEM((LOC, BLK, BLK), BF),
            pltpu.VMEM((tok, FEAT), BF),
            pltpu.VMEM((FEAT, FEAT), BF),
            pltpu.VMEM((FEAT, FEAT), BF),
            pltpu.VMEM((FEAT, FEAT), BF),
            pltpu.VMEM((FEAT, FEAT), BF),
            pltpu.VMEM((BLK, BLK), BF),
            pltpu.VMEM((tc, FEAT), BF),
            pltpu.VMEM((CHUNKS, NM, tc, 128), BF),
            pltpu.VMEM((CHUNKS, NM, tc, 128), BF),
            pltpu.VMEM((CHUNKS, NM, tc, 128), BF),
            pltpu.VMEM((CHUNKS, NM, tc, 128), BF),
            pltpu.VMEM((2, LOC, NX, 2, HALF * slot, BLK), F32),
            pltpu.VMEM((2, 2, 2, LOC, HALF * slot, BLK), BF),
            pltpu.VMEM((2, 2, 2, LOC, HALF * slot, BLK), BF),
            pltpu.VMEM((2, 2, LOC, HALF * slot, BLK), BF),
            pltpu.VMEM((2, 2, LOC, HALF * slot, BLK), BF),
            pltpu.VMEM((2, LOC, NZ, slot, BLK), F32),
            pltpu.VMEM((2, NZ, LOC * slot, BLK), BF),
            pltpu.VMEM((2, NZ - 1, LOC * slot, BLK), BF),
            pltpu.VMEM((2, LOC * slot, BLK), F32),
            pltpu.VMEM((2, LOC * slot, BLK), F32),
            dma((2, 2, 14)),
            dma((2,)),
            dma((2, CHUNKS, NM - 1)),
            dma((2, CHUNKS, NM - 1)),
            dma((2, 2, 12)),
        ],
        compiler_params=pltpu.CompilerParams(
            collective_id=0, has_side_effects=True, vmem_limit_bytes=60 * 1024 * 1024
        ),
        name="monarch_layer",
    )(tokens, upstream, shard)
    return (mixed, gtok, gfac[0], gfac[1])


def solution(mesh):
    placed = (P("dp", "mp"), P("dp", "mp"), P("mp", "dp", None), P("mp", "dp", None))
    return jax.shard_map(
        on_device, mesh=mesh, in_specs=placed, out_specs=placed, check_vma=False
    )
```

time: 1380 us -> 114 us (0.08)
  waiting for transfers between devices: 859 us -> 0 us
  blocking collectives: 443 us -> 0 us
  Pallas kernels: 0 us -> 106 us
  local copies, waits for them, and re-layouts: 23.9 us -> 5.4 us
  between operations: 14.8 us -> 0.65 us
    unnamed x2 -> x0, waiting for transfers between devices: 835 us -> none
    all_gather x2 -> x0, blocking collectives: 443 us -> none  [the longest x1 229 us: on_device(): lax.all_gather(second_factor, 'dp', axis=1, tiled=True)]
    pallas_call x0 -> x1, Pallas kernels: none -> 106 us  [on_device(): pl.pallas_call(functools.partial(kernel, scale), out_shape=(jax.ShapeDtyp...]
    all_to_all x2 -> x0, waiting for transfers between devices: 24.4 us -> none  [the longest x1 24.4 us: on_device(): lax.all_to_all(returning, 'mp', split_axis=0, concat_axis=0, tiled=True)]
  transfers between devices with their start and end apart: 3 -> 0, of which waited for: 2 -> 0; matrix products, arithmetic and copies ran while one was open for 2% -> 0% of each run, Pallas kernels for 0% -> 0%
where the time goes in v2:
time: 114 us; the launch traced here: 112 us
  Pallas kernels  106 us (93%)
  local copies, waits for them, and re-layouts  5.4 us (5%)
    pallas_call x1, Pallas kernels, on_device(): pl.pallas_call(functools.partial(kernel, scale), out_shape=(jax.ShapeDtyp...  106 us
    unnamed x6, local copies, waits for them, and re-layouts  3.33 us

profile of v2, /device:TPU:6, one launch (start us, length us, event | category | flops | bytes accessed | tf_op | source)
XLA Modules:
  0.0 112.3 jit_solution(3719927324610788623)
XLA Ops:
  0.6 0.0 copy-start.1
  0.6 0.7 stack.9
  1.4 0.0 copy-done.1
  1.4 0.6 pad_maximum_fusion.shard_ref
  2.0 105.6 %monarch_layer.1 = (bf16[512,1024]{1,0:T(8,128)(2,1)}, bf16[512,1024]{1,0:T(8,128)(2,1)}, f32[2,4,4,256]{3,2,1,0:T(4,128)}) custom-call(bf16[512,1024]{1,0:T(8,128)(2,1)} %x_ref.1, bf16[512,1024]{1,0:T(8,128)(2,1)} %up_ref.1, bf16[2,16,256]{2,1,0:T(8,128)(2,1)} %pad_maximum_fusion.shard_ref), custom_call_target="tpu_custom_call" | custom-call | tf_op jit(solution)/shard_map/monarch_layer/pallas_call | solution.py:334
  107.6 1.3 %slice_bitcast_fusion = (f32[4,4,256]{2,1,0:T(4,128)}, f32[4,4,256]{2,1,0:T(4,128)}) fusion(f32[2,4,4,256]{3,2,1,0:T(4,128)} %get-tuple-element.9), kind=kLoop, calls=%fused_computation.1 | loop fusion | bytes 65536 | tf_op jit(solution)/shard_map/squeeze | solution.py:379
  109.0 0.0 copy-start
  109.0 2.4 %copy.10 = bf16[512,1024]{1,0:T(8,128)(2,1)} copy(bf16[512,1024]{1,0:T(8,128)(2,1)} %get-tuple-element.16) | data formatting | bytes 2097152
  111.3 0.0 copy-done
  111.3 1.0 copy.11
  (1 shorter events, 0.0 us)
Async XLA Ops:
  0.6 0.7 copy-start.1
  109.0 2.4 %copy-start = (bf16[512,1024]{1,0:T(8,128)(2,1)S(1)}, bf16[512,1024]{1,0:T(8,128)(2,1)}, u32[]{:S(2)}) copy-start(bf16[512,1024]{1,0:T(8,128)(2,1)} %get-tuple-element.17) | copy-start | bytes 3145732

commit v3 on v2

--- a/solution.py
+++ b/solution.py
@@ -12,6 +12,7 @@
 LOC = 4
 ROWS = 4
 NZ, NH, NX = 8, 2, 4
+DP = NZ * NH * NX
 NY, NC = 4, 2
 NM = NY * NC
 FEAT = LOC * BLK
@@ -70,12 +71,12 @@
 
 
 def kernel(
-    scale, x_ref, up_ref, shard_ref,
-    mixed_ref, gtok_ref, gfac_ref,
-    buf, w1, w2, xs, p_send, p_sort, p_nat, p_srt, p_x,
+    scale, x_hbm, up_hbm, first_ref, second_ref,
+    mixed_ref, gtok_ref, gfirst_ref, gsecond_ref,
+    x_ref, up_ref, buf, w1, w2, xs, p_send, p_sort, p_nat, p_srt, p_x,
     u_tmp, send_a, recv_a, send_b, recv_b,
-    g, s1, r1, s2, r2, t, s3, r3, s4, r4,
-    gsem, lsem, sem_a, sem_b, rsem,
+    g, s1, r1, s2, r2, t, s3, r3, s4, r4, s5, r5,
+    lsem, gsem, sem_a, sem_b, rsem, fsem,
 ):
     me, mp = lax.axis_index("dp"), lax.axis_index("mp")
     z, h, x = me // (NH * NX), (me // NX) % NH, me % NX
@@ -101,11 +102,9 @@
             device_id={"mp": mates[k]}, device_id_type=MESH,
         )
 
-    def own(f):
-        return pltpu.make_async_copy(shard_ref.at[f], buf.at[f, x, z, h], lsem.at[f])
-
     def gather_h(f):
-        return push(shard_ref.at[f], buf.at[f, x, z, h], gsem.at[f], 0, to_y)
+        part = buf.at[f, x, z, h]
+        return push(part, part, gsem.at[f], 0, to_y)
 
     def gather_z(f):
         part = buf.at[f, x, z]
@@ -129,8 +128,13 @@
         for c in copies:
             c.wait()
 
-    for f in range(2):
-        own(f).start()
+    load_x = pltpu.make_async_copy(x_hbm, x_ref, lsem.at[0])
+    load_up = pltpu.make_async_copy(up_hbm, up_ref, lsem.at[1])
+    load_x.start()
+    load_up.start()
+    for f, ref in enumerate((first_ref, second_ref)):
+        rows = [ref[b].astype(F32) for b in range(LOC)]
+        buf[f, x, z, h] = jnp.concatenate(rows, axis=0).astype(BF)
     barrier = pltpu.get_barrier_semaphore()
     for peer in [to_y, to_near, to_far] + to_z:
         pl.semaphore_signal(barrier, inc=1, device_id={"dp": peer}, device_id_type=MESH)
@@ -139,8 +143,6 @@
     pl.semaphore_wait(barrier, 3 + len(to_z) + len(mates))
     for f in range(2):
         gather_h(f).start()
-    for f in range(2):
-        own(f).wait()
     write_perm(p_x, natural_of_sorted)
     for f in range(2):
         gather_h(f).wait()
@@ -171,6 +173,7 @@
             dest[b] = nn(perm[b * BLK : (b + 1) * BLK, :], rows).astype(BF)
 
     sort_rows(0, p_nat, w1)
+    load_x.wait()
 
     def chunk(c):
         return pl.ds(pl.multiple_of(c * tc, tc), tc)
@@ -226,6 +229,7 @@
     for c in first + relay:
         c.wait_send()
     sort_rows(1, p_srt, w2)
+    load_up.wait()
 
     @pl.loop(0, CHUNKS)
     def _(c):
@@ -244,77 +248,112 @@
 
     peer = (to_near, to_far)
 
-    def sum_x1(f, k):
-        return push(s1.at[f, k], r1.at[f, k], rsem.at[f], k, peer[k])
-
-    def sum_x2(f, k):
-        return push(s2.at[f, k], r2.at[f, k], rsem.at[f], 2 + k, peer[1 - k])
-
-    def sum_z(f):
-        return [push(s3.at[f, (z + k) % NZ], r3.at[f, k - 1], rsem.at[f], 3 + k, to_z[k - 1]) for k in range(1, NZ)]
-
-    def sum_h(f):
-        return push(s4.at[f], r4.at[f], rsem.at[f], 11, to_y)
-
-    def reduce_x1(f):
+    def sum_x1(k):
+        return push(s1.at[k], r1.at[k], rsem, k, peer[k])
+
+    def sum_x2(k):
+        return push(s2.at[k], r2.at[k], rsem, 2 + k, peer[1 - k])
+
+    def sum_z():
+        return [push(s3.at[(z + k) % NZ], r3.at[k - 1], rsem, 3 + k, to_z[k - 1]) for k in range(1, NZ)]
+
+    def sum_h():
+        return push(s4, r4, rsem, 11, to_y)
+
+    def reduce_x1():
         for k in range(2):
-            s1[f, k, 0] = g[f, :, (near, far)[k], k].astype(BF)
-            s1[f, k, 1] = g[f, :, opp, k].astype(BF)
-            sum_x1(f, k).start()
-
-    def reduce_x2(f):
+            s1[k, 0] = g[1, :, (near, far)[k], k].astype(BF)
+            s1[k, 1] = g[1, :, opp, k].astype(BF)
+            sum_x1(k).start()
+
+    def reduce_x2():
         for k in range(2):
-            sum_x1(f, k).wait_recv()
-            s2[f, k] = (g[f, :, (far, near)[k], k] + r1[f, k, 1].astype(F32)).astype(BF)
-            sum_x2(f, k).start()
-
-    def reduce_z(f):
+            sum_x1(k).wait_recv()
+            s2[k] = (g[1, :, (far, near)[k], k] + r1[k, 1].astype(F32)).astype(BF)
+            sum_x2(k).start()
+
+    def reduce_z():
         for k in range(2):
-            sum_x2(f, k).wait_recv()
-            part = g[f, :, x, k] + r1[f, k, 0].astype(F32) + r2[f, k].astype(F32)
-            t[f, :, k * HALF : (k + 1) * HALF] = part.reshape(LOC, HALF, NH * ROWS, BLK)
+            sum_x2(k).wait_recv()
+            part = g[1, :, x, k] + r1[k, 0].astype(F32) + r2[k].astype(F32)
+            t[:, k * HALF : (k + 1) * HALF] = part.reshape(LOC, HALF, NH * ROWS, BLK)
         for k in range(NZ):
-            s3[f, k] = t[f, :, k].reshape(LOC * NH * ROWS, BLK).astype(BF)
-        start(sum_z(f))
-
-    def reduce_h(f):
-        total = t[f, :, z].reshape(LOC * NH * ROWS, BLK)
-        copies = sum_z(f)
+            s3[k] = t[:, k].reshape(LOC * NH * ROWS, BLK).astype(BF)
+        start(sum_z())
+
+    def reduce_h():
+        total = t[:, z].reshape(LOC * NH * ROWS, BLK)
+        copies = sum_z()
         for k in range(NZ - 1):
             copies[k].wait_recv()
-            total = total + r3[f, k].astype(F32)
-        s4[f] = total
-        sum_h(f).start()
-
-    def reduce_end(f):
-        sum_h(f).wait_recv()
-        total = ((s4[f] + r4[f]) * scale).reshape(LOC, NH * ROWS, BLK)
-        gfac_ref[f] = jnp.where(h == 0, total[:, :ROWS], total[:, ROWS:])
+            total = total + r3[k].astype(F32)
+        total = total.reshape(LOC, NH * ROWS, BLK)
+        s4[...] = jnp.where(h == 0, total[:, ROWS:], total[:, :ROWS])
+        gsecond_ref[...] = jnp.where(h == 0, total[:, :ROWS], total[:, ROWS:])
+        sum_h().start()
+
+    def reduce_end():
+        sum_h().wait_recv()
+        gsecond_ref[...] = (gsecond_ref[...] + r4[...]) * scale
         for k in range(2):
-            sum_x1(f, k).wait_send()
-            sum_x2(f, k).wait_send()
-        for c in sum_z(f):
+            sum_x1(k).wait_send()
+            sum_x2(k).wait_send()
+        for c in sum_z():
             c.wait_send()
-        sum_h(f).wait_send()
-
-    reduce_x1(1)
-
-    @pl.loop(0, CHUNKS)
-    def _(c):
+        sum_h().wait_send()
+
+    def final(i):
+        to = (me + i) % DP
+        return push(s5.at[to], r5.at[i - 1], fsem, i - 1, to)
+
+    def pack_final():
+        low = lax.broadcasted_iota(jnp.int32, (NZ, NH * ROWS, BLK), 1) < ROWS
+        for xx in range(NX):
+            tile = [g[0, b, xx].reshape(NZ, NH * ROWS, BLK) for b in range(LOC)]
+            turned = [pltpu.roll(v, ROWS, 1) for v in tile]
+            for hh in range(NH):
+                pair = []
+                for b in (0, 2):
+                    if hh == 0:
+                        pair.append(jnp.where(low, tile[b], turned[b + 1]))
+                    else:
+                        pair.append(jnp.where(low, turned[b], tile[b + 1]))
+                rows = jnp.concatenate(pair, axis=1).astype(BF)
+                for zz in range(NZ):
+                    s5[dp_of(zz, hh, xx)] = rows[zz]
+
+    reduce_x1()
+
+    def first_grad(c):
         at = chunk(c)
         arrived = collect(recv_b, send_b, sem_b, c)
         for b in range(LOC):
             du = nt(arrived, p_send[block(b), :]).astype(BF)
+            u_tmp[:, block(b)] = du
             g[0, b] += tn(xs[at, block(b)], du).reshape(NX, 2, 32, BLK)
-            back = nt(du, w1[b])
+
+    def token_grad(c):
+        at = chunk(c)
+        for b in range(LOC):
+            back = nt(u_tmp[:, block(b)], w1[b])
             gtok_ref[at, block(b)] = (up_ref[at, block(b)].astype(F32) + back).astype(BF)
+
+    @pl.loop(0, CHUNKS - 1)
+    def _(c):
+        first_grad(c)
+        token_grad(c)
         for step, run in enumerate((reduce_x2, reduce_z, reduce_h)):
-            pl.when(c == step)(functools.partial(run, 1))
-
-    for run in (reduce_x1, reduce_x2, reduce_z, reduce_h):
-        run(0)
-    reduce_end(1)
-    reduce_end(0)
+            pl.when(c == step)(run)
+
+    first_grad(CHUNKS - 1)
+    pack_final()
+
+    @pl.loop(1, DP)
+    def _(i):
+        final(i).start()
+
+    token_grad(CHUNKS - 1)
+    reduce_end()
 
     @pl.loop(0, CHUNKS)
     def _(c):
@@ -322,25 +361,40 @@
             swap(send_a.at[c, mates[k]], recv_a.at[c, mp], sem_a, c, k).wait_send()
             swap(send_b.at[c, mates[k]], recv_b.at[c, mp], sem_b, c, k).wait_send()
 
+    def add_final(i, total):
+        final(i).wait_recv()
+        return total + r5[i - 1].astype(F32)
+
+    total = lax.fori_loop(1, DP, add_final, s5[me].astype(F32)) * scale
+    for b in range(LOC):
+        gfirst_ref[b] = total[b * ROWS : (b + 1) * ROWS]
+
+    @pl.loop(1, DP)
+    def _(i):
+        final(i).wait_send()
+
 
 def on_device(tokens, upstream, first_factor, second_factor):
     tok = tokens.shape[0]
     tc = tok // CHUNKS
     scale = 1.0 / math.sqrt(tok * lax.axis_size("dp"))
-    shard = jnp.stack([first_factor, second_factor]).reshape(2, LOC * ROWS, BLK)
     vmem = pl.BlockSpec(memory_space=pltpu.VMEM)
+    hbm = pl.BlockSpec(memory_space=pltpu.HBM)
     dma = pltpu.SemaphoreType.DMA
     slot = NH * ROWS
-    mixed, gtok, gfac = pl.pallas_call(
+    return pl.pallas_call(
         functools.partial(kernel, scale),
         out_shape=(
             jax.ShapeDtypeStruct((tok, FEAT), BF),
             jax.ShapeDtypeStruct((tok, FEAT), BF),
-            jax.ShapeDtypeStruct((2, LOC, ROWS, BLK), F32),
+            jax.ShapeDtypeStruct((LOC, ROWS, BLK), F32),
+            jax.ShapeDtypeStruct((LOC, ROWS, BLK), F32),
         ),
-        in_specs=[vmem, vmem, vmem],
-        out_specs=(vmem, vmem, vmem),
+        in_specs=[hbm, hbm, vmem, vmem],
+        out_specs=(vmem,) * 4,
         scratch_shapes=[
+            pltpu.VMEM((tok, FEAT), BF),
+            pltpu.VMEM((tok, FEAT), BF),
             pltpu.VMEM((2, NX, NZ, NH, LOC * ROWS, BLK), BF),
             pltpu.VMEM((LOC, BLK, BLK), BF),
             pltpu.VMEM((LOC, BLK, BLK), BF),
@@ -356,27 +410,29 @@
             pltpu.VMEM((CHUNKS, NM, tc, 128), BF),
             pltpu.VMEM((CHUNKS, NM, tc, 128), BF),
             pltpu.VMEM((2, LOC, NX, 2, HALF * slot, BLK), F32),
-            pltpu.VMEM((2, 2, 2, LOC, HALF * slot, BLK), BF),
-            pltpu.VMEM((2, 2, 2, LOC, HALF * slot, BLK), BF),
             pltpu.VMEM((2, 2, LOC, HALF * slot, BLK), BF),
             pltpu.VMEM((2, 2, LOC, HALF * slot, BLK), BF),
-            pltpu.VMEM((2, LOC, NZ, slot, BLK), F32),
-            pltpu.VMEM((2, NZ, LOC * slot, BLK), BF),
-            pltpu.VMEM((2, NZ - 1, LOC * slot, BLK), BF),
-            pltpu.VMEM((2, LOC * slot, BLK), F32),
-            pltpu.VMEM((2, LOC * slot, BLK), F32),
+            pltpu.VMEM((2, LOC, HALF * slot, BLK), BF),
+            pltpu.VMEM((2, LOC, HALF * slot, BLK), BF),
+            pltpu.VMEM((LOC, NZ, slot, BLK), F32),
+            pltpu.VMEM((NZ, LOC * slot, BLK), BF),
+            pltpu.VMEM((NZ - 1, LOC * slot, BLK), BF),
+            pltpu.VMEM((LOC, ROWS, BLK), F32),
+            pltpu.VMEM((LOC, ROWS, BLK), F32),
+            pltpu.VMEM((DP, LOC * ROWS, BLK), BF),
+            pltpu.VMEM((DP - 1, LOC * ROWS, BLK), BF),
+            dma((2,)),
             dma((2, 2, 14)),
-            dma((2,)),
             dma((2, CHUNKS, NM - 1)),
             dma((2, CHUNKS, NM - 1)),
-            dma((2, 2, 12)),
+            dma((2, 12)),
+            dma((2, DP - 1)),
         ],
         compiler_params=pltpu.CompilerParams(
-            collective_id=0, has_side_effects=True, vmem_limit_bytes=60 * 1024 * 1024
+            collective_id=0, has_side_effects=True, vmem_limit_bytes=40 * 1024 * 1024
         ),
         name="monarch_layer",
-    )(tokens, upstream, shard)
-    return (mixed, gtok, gfac[0], gfac[1])
+    )(tokens, upstream, first_factor, second_factor)
 
 
 def solution(mesh):

time: 114 us -> 114 us (level)
  Pallas kernels: 106 us -> 104 us
  local copies, waits for them, and re-layouts: 5.4 us -> 6.99 us
    unnamed x6 -> x12, local copies, waits for them, and re-layouts: 3.33 us -> 6.99 us
    pallas_call x1, Pallas kernels: 106 us -> 104 us  [on_device(): pl.pallas_call(functools.partial(kernel, scale), out_shape=(jax.ShapeDtyp...]
    squeeze x1 -> x0, local copies, waits for them, and re-layouts: 1.35 us -> none  [on_device(): return (mixed, gtok, gfac[0], gfac[1])]
where the time goes in v3:
time: 114 us; the launch traced here: 112 us
  Pallas kernels  104 us (91%)
  local copies, waits for them, and re-layouts  6.99 us (6%)
    pallas_call x1, Pallas kernels, on_device(): pl.pallas_call(functools.partial(kernel, scale), out_shape=(jax.ShapeDtyp...  104 us
    unnamed x12, local copies, waits for them, and re-layouts  6.99 us

profile of v3, /device:TPU:6, one launch (start us, length us, event | category | flops | bytes accessed | tf_op | source)
XLA Modules:
  0.0 111.7 jit_solution(17727504819304822639)
XLA Ops:
  0.6 0.0 copy-start
  0.6 1.2 %copy-done = bf16[512,1024]{1,0:T(8,128)(2,1)S(1)} copy-done((bf16[512,1024]{1,0:T(8,128)(2,1)S(1)}, bf16[512,1024]{1,0:T(8,128)(2,1)}, u32[]{:S(2)}) %copy-start) | copy-done | bytes 1048600
  1.9 0.0 copy-start.1
  1.9 1.2 %copy-done.1 = bf16[512,1024]{1,0:T(8,128)(2,1)S(1)} copy-done((bf16[512,1024]{1,0:T(8,128)(2,1)S(1)}, bf16[512,1024]{1,0:T(8,128)(2,1)}, u32[]{:S(2)}) %copy-start.1) | copy-done | bytes 1048600
  3.1 0.0 copy-start.2
  3.1 0.7 copy-done.2
  3.8 0.0 copy-start.3
  3.8 0.7 copy-done.3
  4.5 104.0 %monarch_layer.1 = (bf16[512,1024]{1,0:T(8,128)(2,1)S(1)}, bf16[512,1024]{1,0:T(8,128)(2,1)S(1)}, f32[4,4,256]{2,1,0:T(4,128)S(1)}, f32[4,4,256]{2,1,0:T(4,128)S(1)}) custom-call(bf16[512,1024]{1,0:T(8,128)(2,1)S(1)} %copy-done, bf16[512,1024]{1,0:T(8,128)(2,1)S(1)} %copy-done.1, bf16[4,4,256]{2,1,0:T(4,128)(2,1)S(1)} %copy-done.2, ...), custom_call_target="tpu_custom_call" | custom-call | tf_op jit(solution)/shard_map/monarch_layer/pallas_call | solution.py:385
  108.5 1.0 copy.12
  109.5 1.0 copy.13
  110.5 0.6 copy.14
  111.1 0.6 copy.15
Async XLA Ops:
  0.6 1.2 %copy-start = (bf16[512,1024]{1,0:T(8,128)(2,1)S(1)}, bf16[512,1024]{1,0:T(8,128)(2,1)}, u32[]{:S(2)}) copy-start(bf16[512,1024]{1,0:T(8,128)(2,1)} %x_hbm.1) | copy-start | bytes 3145732
  1.9 1.2 %copy-start.1 = (bf16[512,1024]{1,0:T(8,128)(2,1)S(1)}, bf16[512,1024]{1,0:T(8,128)(2,1)}, u32[]{:S(2)}) copy-start(bf16[512,1024]{1,0:T(8,128)(2,1)} %up_hbm.1) | copy-start | bytes 3145732
  3.1 0.7 copy-start.2
  3.8 0.7 copy-start.3

commit v4 on v3

--- a/solution.py
+++ b/solution.py
@@ -39,7 +39,7 @@
 
 
 def natural_of_send(s):
-    return ((s >> 5) & 3) * 256 + (s >> 7) * 32 + (s & 31)
+    return ((s >> 5) & 3) * 128 + (s >> 7) * 32 + (s & 31)
 
 
 def arrived_of_sorted(v):
@@ -71,9 +71,9 @@
 
 
 def kernel(
-    scale, x_hbm, up_hbm, first_ref, second_ref,
+    scale, x_hbm, up_hbm, first_hbm, second_hbm,
     mixed_ref, gtok_ref, gfirst_ref, gsecond_ref,
-    x_ref, up_ref, buf, w1, w2, xs, p_send, p_sort, p_nat, p_srt, p_x,
+    x_ref, up_ref, shard, buf_a, buf_b, w1, w2, xs, p_send, p_sort, p_nat, p_srt, p_x,
     u_tmp, send_a, recv_a, send_b, recv_b,
     g, s1, r1, s2, r2, t, s3, r3, s4, r4, s5, r5,
     lsem, gsem, sem_a, sem_b, rsem, fsem,
@@ -102,23 +102,52 @@
             device_id={"mp": mates[k]}, device_id_type=MESH,
         )
 
+    bufs = (buf_a.at[0], buf_a.at[1], buf_b)
+    sides = (1 - yl // 2, yl // 2)
+
     def gather_h(f):
-        part = buf.at[f, x, z, h]
+        part = bufs[f].at[x, z, h]
         return push(part, part, gsem.at[f], 0, to_y)
 
     def gather_z(f):
-        part = buf.at[f, x, z]
+        part = bufs[f].at[x, z]
         return [push(part, part, gsem.at[f], k, to_z[k - 1]) for k in range(1, NZ)]
 
     def gather_x(f):
         halves = [pl.ds(0, HALF), pl.ds(HALF, HALF)]
 
         def one(slot, half, k, peer):
-            part = buf.at[f, slot, halves[half]]
+            part = bufs[f].at[slot, halves[half]]
             return push(part, part, gsem.at[f], k, peer)
 
-        first = [one(x, 0, 8, to_near), one(x, 1, 9, to_far), one(x, 1, 10, to_near), one(x, 0, 11, to_far)]
-        return first, lambda: [one(near, 0, 12, to_far), one(far, 1, 13, to_near)]
+        def first():
+            return [one(x, 0, 8, to_near), one(x, 1, 9, to_far)]
+
+        def second():
+            return [one(x, 1, 10, to_near), one(x, 0, 11, to_far)]
+
+        def relay():
+            return [one(near, 0, 12, to_far), one(far, 1, 13, to_near)]
+
+        return first, second, relay
+
+    def open_x(f):
+        first, second, _ = gather_x(f)
+        start(first() + second())
+
+    def relay_x(f):
+        first, _, relay = gather_x(f)
+        for c, onward in zip(first(), relay()):
+            c.wait_recv()
+            onward.start()
+
+    def close_x(f):
+        first, second, relay = gather_x(f)
+        rest = second() + relay()
+        for c in rest:
+            c.wait_recv()
+        for c in first() + rest:
+            c.wait_send()
 
     def start(copies):
         for c in copies:
@@ -130,50 +159,55 @@
 
     load_x = pltpu.make_async_copy(x_hbm, x_ref, lsem.at[0])
     load_up = pltpu.make_async_copy(up_hbm, up_ref, lsem.at[1])
+    load_rows = [
+        pltpu.make_async_copy(ref, shard.at[f], lsem.at[2 + f])
+        for f, ref in enumerate((first_hbm, second_hbm))
+    ]
+    start(load_rows)
     load_x.start()
     load_up.start()
-    for f, ref in enumerate((first_ref, second_ref)):
-        rows = [ref[b].astype(F32) for b in range(LOC)]
-        buf[f, x, z, h] = jnp.concatenate(rows, axis=0).astype(BF)
+    wait(load_rows)
+    for f in range(2):
+        rows = [shard[f, b].astype(F32) for b in range(LOC)]
+        rows = jnp.concatenate(rows, axis=0)
+        if f == 1:
+            buf_b[x, z, h] = rows.astype(BF)
+        else:
+            low, high = rows[:, :128], rows[:, 128:]
+            buf_a[0, x, z, h] = jnp.where(yl < NY // 2, high, low).astype(BF)
+            buf_a[1, x, z, h] = jnp.where(yl < NY // 2, low, high).astype(BF)
     barrier = pltpu.get_barrier_semaphore()
     for peer in [to_y, to_near, to_far] + to_z:
         pl.semaphore_signal(barrier, inc=1, device_id={"dp": peer}, device_id_type=MESH)
     for mate in mates:
         pl.semaphore_signal(barrier, inc=1, device_id={"mp": mate}, device_id_type=MESH)
     pl.semaphore_wait(barrier, 3 + len(to_z) + len(mates))
-    for f in range(2):
+    for f in range(3):
         gather_h(f).start()
     write_perm(p_x, natural_of_sorted)
-    for f in range(2):
+    for f in range(3):
         gather_h(f).wait()
         start(gather_z(f))
     write_perm(p_nat, natural_of_gathered)
     write_perm(p_send, natural_of_send)
     wait(gather_z(0))
-    first, relays = gather_x(0)
-    relay = relays()
-    start(first)
+    open_x(0)
+    wait(gather_z(1))
     write_perm(p_sort, arrived_of_sorted)
-    for k in range(2):
-        first[k].wait_recv()
-        relay[k].start()
+    relay_x(0)
+    open_x(1)
     write_perm(p_srt, sorted_of_gathered)
     g[...] = jnp.zeros_like(g)
-    for k in range(2):
-        first[2 + k].wait_recv()
-        relay[k].wait_recv()
-    for c in first + relay:
-        c.wait_send()
-    wait(gather_z(1))
-    start(gather_x(1)[0])
-
-    def sort_rows(f, perm, dest):
-        rows = buf[f].reshape(FEAT, BLK)
+    load_x.wait()
+    close_x(0)
+
+    def side_lanes(p):
+        return pl.ds(pl.multiple_of(sides[p] * 128, 128), 128)
+
+    def sort_first(p):
+        rows = buf_a[p].reshape(FEAT, 128)
         for b in range(LOC):
-            dest[b] = nn(perm[b * BLK : (b + 1) * BLK, :], rows).astype(BF)
-
-    sort_rows(0, p_nat, w1)
-    load_x.wait()
+            w1[b, :, side_lanes(p)] = nn(p_nat[b * BLK : (b + 1) * BLK, :], rows).astype(BF)
 
     def chunk(c):
         return pl.ds(pl.multiple_of(c * tc, tc), tc)
@@ -181,11 +215,12 @@
     def block(b):
         return slice(b * BLK, (b + 1) * BLK)
 
-    def spread(values, send, recv, sems, c):
-        for n in range(NM):
-            send[c, n] = values(n)
-        for k in range(NM - 1):
+    def launch(send, recv, sems, c, ks):
+        for k in ks:
             swap(send.at[c, mates[k]], recv.at[c, mp], sems, c, k).start()
+
+    def launch_all(send, recv, sems, c):
+        launch(send, recv, sems, c, range(NM - 1))
         recv[c, mp] = send[c, mp]
 
     def collect(recv, send, sems, c):
@@ -193,42 +228,49 @@
             swap(send.at[c, mates[k]], recv.at[c, mates[k]], sems, c, k).wait_recv()
         return jnp.concatenate([recv[c, n] for n in range(NM)], axis=1)
 
-    def permuted_send(perm_tile, send, recv, sems, c):
-        done = {}
-
-        def lanes(n):
-            if n % 2 == 0:
-                done[0] = perm_tile(n // 2).astype(BF)
-            return done[0][:, (n % 2) * 128 : (n % 2 + 1) * 128]
-
-        spread(lanes, send, recv, sems, c)
-
-    @pl.loop(0, CHUNKS)
+    def send_side(half, side, c):
+        lanes = nn(half, p_send[...]).astype(BF)
+        for n in range(NM // 2):
+            send_a[c, side * (NM // 2) + n] = lanes[:, n * 128 : (n + 1) * 128]
+
+    for p in range(2):
+        if p == 1:
+            relay_x(1)
+            wait(gather_z(2))
+            open_x(2)
+            close_x(1)
+        sort_first(p)
+        at = chunk(0)
+        half = [nn(x_ref[at, block(b)], w1[b, :, side_lanes(p)]).astype(BF) for b in range(LOC)]
+        send_side(jnp.concatenate(half, axis=1), sides[p], 0)
+        launch(send_a, recv_a, sem_a, 0, (range(3, NM - 1), range(3))[p])
+    recv_a[0, mp] = send_a[0, mp]
+
+    def sort_tokens(at):
+        for b in range(LOC):
+            xs[at, block(b)] = nn(x_ref[at, block(b)], p_x[...]).astype(BF)
+
+    @pl.loop(1, CHUNKS)
     def _(c):
         at = chunk(c)
         for b in range(LOC):
             u_tmp[:, block(b)] = nn(x_ref[at, block(b)], w1[b]).astype(BF)
-        permuted_send(lambda k: nn(u_tmp[...], p_send[:, block(k)]), send_a, recv_a, sem_a, c)
+        for side in range(2):
+            half = [u_tmp[:, b * BLK + side * 128 : b * BLK + side * 128 + 128] for b in range(LOC)]
+            send_side(jnp.concatenate(half, axis=1), side, c)
+        launch_all(send_a, recv_a, sem_a, c)
 
         @pl.when(c == 1)
         def _():
-            first, relays = gather_x(1)
-            relay = relays()
-            for k in range(2):
-                first[k].wait_recv()
-                relay[k].start()
-
-        for b in range(LOC):
-            xs[at, block(b)] = nn(x_ref[at, block(b)], p_x[...]).astype(BF)
-
-    first, relays = gather_x(1)
-    relay = relays()
-    for k in range(2):
-        first[2 + k].wait_recv()
-        relay[k].wait_recv()
-    for c in first + relay:
-        c.wait_send()
-    sort_rows(1, p_srt, w2)
+            relay_x(2)
+
+        sort_tokens(at)
+
+    sort_tokens(chunk(0))
+    close_x(2)
+    rows = buf_b[...].reshape(FEAT, BLK)
+    for b in range(LOC):
+        w2[b] = nn(p_srt[block(b), :], rows).astype(BF)
     load_up.wait()
 
     @pl.loop(0, CHUNKS)
@@ -244,7 +286,11 @@
             cot = (up_ref[at, block(j)].astype(F32) * slope).astype(BF)
             g[1, j] += tn(v, cot).reshape(NX, 2, 32, BLK)
             u_tmp[:, block(j)] = nt(cot, w2[j]).astype(BF)
-        permuted_send(lambda k: nt(u_tmp[...], p_sort[block(k), :]), send_b, recv_b, sem_b, c)
+        for k in range(LOC):
+            lanes = nt(u_tmp[...], p_sort[block(k), :]).astype(BF)
+            send_b[c, 2 * k] = lanes[:, :128]
+            send_b[c, 2 * k + 1] = lanes[:, 128:]
+        launch_all(send_b, recv_b, sem_b, c)
 
     peer = (to_near, to_far)
 
@@ -327,8 +373,9 @@
     def first_grad(c):
         at = chunk(c)
         arrived = collect(recv_b, send_b, sem_b, c)
+        side = [nt(arrived[:, k * 512 : (k + 1) * 512], p_send[...]).astype(BF) for k in range(2)]
         for b in range(LOC):
-            du = nt(arrived, p_send[block(b), :]).astype(BF)
+            du = jnp.concatenate([v[:, b * 128 : (b + 1) * 128] for v in side], axis=1)
             u_tmp[:, block(b)] = du
             g[0, b] += tn(xs[at, block(b)], du).reshape(NX, 2, 32, BLK)
 
@@ -374,15 +421,39 @@
         final(i).wait_send()
 
 
-def on_device(tokens, upstream, first_factor, second_factor):
-    tok = tokens.shape[0]
+def store_kernel(*refs):
+    count = len(refs) // 2
+    sems = refs[-1]
+    copies = [
+        pltpu.make_async_copy(refs[i], refs[count + i], sems.at[i]) for i in range(count)
+    ]
+    for c in copies:
+        c.start()
+    for c in copies:
+        c.wait()
+
+
+def store(results):
+    count = len(results)
+    return pl.pallas_call(
+        store_kernel,
+        out_shape=tuple(jax.ShapeDtypeStruct(r.shape, r.dtype) for r in results),
+        in_specs=[pl.BlockSpec(memory_space=pltpu.VMEM)] * count,
+        out_specs=(pl.BlockSpec(memory_space=pltpu.HBM),) * count,
+        scratch_shapes=[pltpu.SemaphoreType.DMA((count,))],
+        name="store_results",
+    )(*(pltpu.with_memory_space_constraint(r, pltpu.VMEM) for r in results))
+
+
+def on_device(*args):
+    tok = args[0].shape[0]
     tc = tok // CHUNKS
     scale = 1.0 / math.sqrt(tok * lax.axis_size("dp"))
     vmem = pl.BlockSpec(memory_space=pltpu.VMEM)
     hbm = pl.BlockSpec(memory_space=pltpu.HBM)
     dma = pltpu.SemaphoreType.DMA
     slot = NH * ROWS
-    return pl.pallas_call(
+    results = pl.pallas_call(
         functools.partial(kernel, scale),
         out_shape=(
             jax.ShapeDtypeStruct((tok, FEAT), BF),
@@ -390,16 +461,18 @@
             jax.ShapeDtypeStruct((LOC, ROWS, BLK), F32),
             jax.ShapeDtypeStruct((LOC, ROWS, BLK), F32),
         ),
-        in_specs=[hbm, hbm, vmem, vmem],
+        in_specs=[hbm] * 4,
         out_specs=(vmem,) * 4,
         scratch_shapes=[
             pltpu.VMEM((tok, FEAT), BF),
             pltpu.VMEM((tok, FEAT), BF),
-            pltpu.VMEM((2, NX, NZ, NH, LOC * ROWS, BLK), BF),
+            pltpu.VMEM((2, LOC, ROWS, BLK), BF),
+            pltpu.VMEM((2, NX, NZ, NH, LOC * ROWS, 128), BF),
+            pltpu.VMEM((NX, NZ, NH, LOC * ROWS, BLK), BF),
             pltpu.VMEM((LOC, BLK, BLK), BF),
             pltpu.VMEM((LOC, BLK, BLK), BF),
             pltpu.VMEM((tok, FEAT), BF),
-            pltpu.VMEM((FEAT, FEAT), BF),
+            pltpu.VMEM((FEAT // 2, FEAT // 2), BF),
             pltpu.VMEM((FEAT, FEAT), BF),
             pltpu.VMEM((FEAT, FEAT), BF),
             pltpu.VMEM((FEAT, FEAT), BF),
@@ -421,8 +494,8 @@
             pltpu.VMEM((LOC, ROWS, BLK), F32),
             pltpu.VMEM((DP, LOC * ROWS, BLK), BF),
             pltpu.VMEM((DP - 1, LOC * ROWS, BLK), BF),
-            dma((2,)),
-            dma((2, 2, 14)),
+            dma((4,)),
+            dma((3, 2, 14)),
             dma((2, CHUNKS, NM - 1)),
             dma((2, CHUNKS, NM - 1)),
             dma((2, 12)),
@@ -432,7 +505,8 @@
             collective_id=0, has_side_effects=True, vmem_limit_bytes=40 * 1024 * 1024
         ),
         name="monarch_layer",
-    )(tokens, upstream, first_factor, second_factor)
+    )(*(pltpu.with_memory_space_constraint(v, pltpu.HBM) for v in args))
+    return store(results)
 
 
 def solution(mesh):

time: 114 us -> 106 us (0.930)
  local copies, waits for them, and re-layouts: 6.99 us -> 0 us
    unnamed x12 -> x0, local copies, waits for them, and re-layouts: 6.99 us -> none
    pallas_call x1, Pallas kernels: 104 us -> 102 us  [on_device(): pl.pallas_call(functools.partial(kernel, scale), out_shape=(jax.ShapeDtyp...]
    pallas_call x0 -> x1, Pallas kernels: none -> 1.36 us  [store(): pl.pallas_call(store_kernel, out_shape=tuple((jax.ShapeDtypeStruct(r.shap...]
where the time goes in v4:
time: 106 us; the launch traced here: 104 us
  Pallas kernels  103 us (97%)
    pallas_call x1, Pallas kernels, on_device(): pl.pallas_call(functools.partial(kernel, scale), out_shape=(jax.ShapeDtyp...  102 us

profile of v4, /device:TPU:6, one launch (start us, length us, event | category | flops | bytes accessed | tf_op | source)
XLA Modules:
  0.0 104.0 jit_solution(16922986115278506116)
XLA Ops:
  0.6 102.0 %monarch_layer.1 = (bf16[512,1024]{1,0:T(8,128)(2,1)S(1)}, bf16[512,1024]{1,0:T(8,128)(2,1)S(1)}, f32[4,4,256]{2,1,0:T(4,128)S(1)}, f32[4,4,256]{2,1,0:T(4,128)S(1)}) custom-call(bf16[512,1024]{1,0:T(8,128)(2,1)} %x_hbm.1, bf16[512,1024]{1,0:T(8,128)(2,1)} %up_hbm.1, bf16[4,4,256]{2,1,0:T(4,128)(2,1)} %first_hbm.1, bf16[4,4,256]{2,1,0:T(4,128)(2,1)} %second_hbm.1), custom_call_target="tpu_custom_call" | custom-call | tf_op jit(solution)/shard_map/monarch_layer/pallas_call | solution.py:456
  102.7 1.4 %store_results.1 = (bf16[512,1024]{1,0:T(8,128)(2,1)}, bf16[512,1024]{1,0:T(8,128)(2,1)}, f32[4,4,256]{2,1,0:T(4,128)}, f32[4,4,256]{2,1,0:T(4,128)}) custom-call(bf16[512,1024]{1,0:T(8,128)(2,1)S(1)} %get-tuple-element.8.refs_0_, bf16[512,1024]{1,0:T(8,128)(2,1)S(1)} %get-tuple-element.9.refs_1_, f32[4,4,256]{2,1,0:T(4,128)S(1)} %get-tuple-element.10.refs_2_, ...), custom_call_target="tpu_custom_call" | custom-call | tf_op jit(solution)/shard_map/store_results/pallas_call | solution.py:438

commit v5 on v4

--- a/solution.py
+++ b/solution.py
@@ -83,9 +83,14 @@
     near, far, opp = x + 1 - 2 * (x % 2), NX - 1 - x, (x + 2) % NX
     yl, core = mp // NC, mp % NC
     ys = (yl, yl + 1 - 2 * (yl % 2), NY - 1 - yl, (yl + 2) % NY)
-    mates = [ys[0] * NC + 1 - core]
-    for k in (1, 2, 3):
-        mates += [ys[k] * NC + core, ys[k] * NC + 1 - core]
+    end = ((yl + 1) // 2 + 1) % 2
+    turns = [(3 * end + 2 * (1 - end), ys[2] * end + ys[3] * (1 - end)), (2 * end + 3 * (1 - end), ys[3] * end + ys[2] * (1 - end)), (1, ys[1])]
+    kinds, mates = [], []
+    for kind, row in turns:
+        kinds += [2 * kind - 1, 2 * kind]
+        mates += [row * NC + core, row * NC + 1 - core]
+    kinds.append(0)
+    mates.append(yl * NC + 1 - core)
     to_y, to_near, to_far = dp_of(z, 1 - h, x), dp_of(z, h, near), dp_of(z, h, far)
     to_z = [dp_of((z + k) % NZ, h, x) for k in range(1, NZ)]
     tc = x_ref.shape[0] // CHUNKS
@@ -98,7 +103,8 @@
 
     def swap(src, dst, sems, c, k):
         return pltpu.make_async_remote_copy(
-            src_ref=src, dst_ref=dst, send_sem=sems.at[0, c, k], recv_sem=sems.at[1, c, k],
+            src_ref=src, dst_ref=dst,
+            send_sem=sems.at[0, c, kinds[k]], recv_sem=sems.at[1, c, kinds[k]],
             device_id={"mp": mates[k]}, device_id_type=MESH,
         )
 
@@ -157,6 +163,11 @@
         for c in copies:
             c.wait()
 
+    barrier = pltpu.get_barrier_semaphore()
+    for peer in [to_y, to_near, to_far] + to_z:
+        pl.semaphore_signal(barrier, inc=1, device_id={"dp": peer}, device_id_type=MESH)
+    for mate in mates:
+        pl.semaphore_signal(barrier, inc=1, device_id={"mp": mate}, device_id_type=MESH)
     load_x = pltpu.make_async_copy(x_hbm, x_ref, lsem.at[0])
     load_up = pltpu.make_async_copy(up_hbm, up_ref, lsem.at[1])
     load_rows = [
@@ -176,11 +187,6 @@
             low, high = rows[:, :128], rows[:, 128:]
             buf_a[0, x, z, h] = jnp.where(yl < NY // 2, high, low).astype(BF)
             buf_a[1, x, z, h] = jnp.where(yl < NY // 2, low, high).astype(BF)
-    barrier = pltpu.get_barrier_semaphore()
-    for peer in [to_y, to_near, to_far] + to_z:
-        pl.semaphore_signal(barrier, inc=1, device_id={"dp": peer}, device_id_type=MESH)
-    for mate in mates:
-        pl.semaphore_signal(barrier, inc=1, device_id={"mp": mate}, device_id_type=MESH)
     pl.semaphore_wait(barrier, 3 + len(to_z) + len(mates))
     for f in range(3):
         gather_h(f).start()
@@ -243,7 +249,7 @@
         at = chunk(0)
         half = [nn(x_ref[at, block(b)], w1[b, :, side_lanes(p)]).astype(BF) for b in range(LOC)]
         send_side(jnp.concatenate(half, axis=1), sides[p], 0)
-        launch(send_a, recv_a, sem_a, 0, (range(3, NM - 1), range(3))[p])
+        launch(send_a, recv_a, sem_a, 0, (range(4), range(4, NM - 1))[p])
     recv_a[0, mp] = send_a[0, mp]
 
     def sort_tokens(at):
@@ -348,25 +354,31 @@
             c.wait_send()
         sum_h().wait_send()
 
-    def final(i):
-        to = (me + i) % DP
-        return push(s5.at[to], r5.at[i - 1], fsem, i - 1, to)
-
-    def pack_final():
+    def final(to, slot):
+        return pltpu.make_async_remote_copy(
+            src_ref=s5.at[to], dst_ref=r5.at[slot],
+            send_sem=fsem.at[0, to], recv_sem=fsem.at[1, slot],
+            device_id={"dp": to}, device_id_type=MESH,
+        )
+
+    def send_final(hh):
         low = lax.broadcasted_iota(jnp.int32, (NZ, NH * ROWS, BLK), 1) < ROWS
         for xx in range(NX):
-            tile = [g[0, b, xx].reshape(NZ, NH * ROWS, BLK) for b in range(LOC)]
-            turned = [pltpu.roll(v, ROWS, 1) for v in tile]
-            for hh in range(NH):
-                pair = []
-                for b in (0, 2):
-                    if hh == 0:
-                        pair.append(jnp.where(low, tile[b], turned[b + 1]))
-                    else:
-                        pair.append(jnp.where(low, turned[b], tile[b + 1]))
-                rows = jnp.concatenate(pair, axis=1).astype(BF)
-                for zz in range(NZ):
-                    s5[dp_of(zz, hh, xx)] = rows[zz]
+            pair = []
+            for b in (0, 2):
+                one, two = (g[0, b + k, xx].reshape(NZ, NH * ROWS, BLK) for k in range(2))
+                if hh == 0:
+                    pair.append(jnp.where(low, one, pltpu.roll(two, ROWS, 1)))
+                else:
+                    pair.append(jnp.where(low, pltpu.roll(one, ROWS, 1), two))
+            rows = jnp.concatenate(pair, axis=1).astype(BF)
+            for zz in range(NZ):
+                s5[dp_of(zz, hh, xx)] = rows[zz]
+
+            @pl.loop(0, NZ)
+            def _(zz):
+                to = dp_of(zz, hh, xx)
+                pl.when(to != me)(lambda: final(to, me).start())
 
     reduce_x1()
 
@@ -393,11 +405,12 @@
             pl.when(c == step)(run)
 
     first_grad(CHUNKS - 1)
-    pack_final()
-
-    @pl.loop(1, DP)
-    def _(i):
-        final(i).start()
+    for hh in range(NH):
+
+        @pl.when(h == hh)
+        def _():
+            send_final(1 - hh)
+            send_final(hh)
 
     token_grad(CHUNKS - 1)
     reduce_end()
@@ -409,8 +422,9 @@
             swap(send_b.at[c, mates[k]], recv_b.at[c, mp], sem_b, c, k).wait_send()
 
     def add_final(i, total):
-        final(i).wait_recv()
-        return total + r5[i - 1].astype(F32)
+        peer = (me + i) % DP
+        final(peer, peer).wait_recv()
+        return total + r5[peer].astype(F32)
 
     total = lax.fori_loop(1, DP, add_final, s5[me].astype(F32)) * scale
     for b in range(LOC):
@@ -418,7 +432,8 @@
 
     @pl.loop(1, DP)
     def _(i):
-        final(i).wait_send()
+        peer = (me + i) % DP
+        final(peer, peer).wait_send()
 
 
 def store_kernel(*refs):
@@ -493,13 +508,13 @@
             pltpu.VMEM((LOC, ROWS, BLK), F32),
             pltpu.VMEM((LOC, ROWS, BLK), F32),
             pltpu.VMEM((DP, LOC * ROWS, BLK), BF),
-            pltpu.VMEM((DP - 1, LOC * ROWS, BLK), BF),
+            pltpu.VMEM((DP, LOC * ROWS, BLK), BF),
             dma((4,)),
             dma((3, 2, 14)),
             dma((2, CHUNKS, NM - 1)),
             dma((2, CHUNKS, NM - 1)),
             dma((2, 12)),
-            dma((2, DP - 1)),
+            dma((2, DP)),
         ],
         compiler_params=pltpu.CompilerParams(
             collective_id=0, has_side_effects=True, vmem_limit_bytes=40 * 1024 * 1024

time: 106 us -> 103 us (0.972)
  the two profiles are of different devices: /device:TPU:6 before, /device:TPU:14 now
where the time goes in v5:
time: 103 us
  Pallas kernels  102 us (99%)
    pallas_call x1, Pallas kernels, on_device(): pl.pallas_call(functools.partial(kernel, scale), out_shape=(jax.ShapeDtyp...  101 us

profile of v5, /device:TPU:14, one launch (start us, length us, event | category | flops | bytes accessed | tf_op | source)
XLA Modules:
  0.0 103.0 jit_solution(6890833523663898155)
XLA Ops:
  0.6 101.0 %monarch_layer.1 = (bf16[512,1024]{1,0:T(8,128)(2,1)S(1)}, bf16[512,1024]{1,0:T(8,128)(2,1)S(1)}, f32[4,4,256]{2,1,0:T(4,128)S(1)}, f32[4,4,256]{2,1,0:T(4,128)S(1)}) custom-call(bf16[512,1024]{1,0:T(8,128)(2,1)} %x_hbm.1, bf16[512,1024]{1,0:T(8,128)(2,1)} %up_hbm.1, bf16[4,4,256]{2,1,0:T(4,128)(2,1)} %first_hbm.1, bf16[4,4,256]{2,1,0:T(4,128)(2,1)} %second_hbm.1), custom_call_target="tpu_custom_call" | custom-call | tf_op jit(solution)/shard_map/monarch_layer/pallas_call | solution.py:471
  101.6 1.4 %store_results.1 = (bf16[512,1024]{1,0:T(8,128)(2,1)}, bf16[512,1024]{1,0:T(8,128)(2,1)}, f32[4,4,256]{2,1,0:T(4,128)}, f32[4,4,256]{2,1,0:T(4,128)}) custom-call(bf16[512,1024]{1,0:T(8,128)(2,1)S(1)} %get-tuple-element.8.refs_0_, bf16[512,1024]{1,0:T(8,128)(2,1)S(1)} %get-tuple-element.9.refs_1_, f32[4,4,256]{2,1,0:T(4,128)S(1)} %get-tuple-element.10.refs_2_, ...), custom_call_target="tpu_custom_call" | custom-call | tf_op jit(solution)/shard_map/store_results/pallas_call | solution.py:453

commit v6 on v5

--- a/solution.py
+++ b/solution.py
@@ -75,8 +75,8 @@
     mixed_ref, gtok_ref, gfirst_ref, gsecond_ref,
     x_ref, up_ref, shard, buf_a, buf_b, w1, w2, xs, p_send, p_sort, p_nat, p_srt, p_x,
     u_tmp, send_a, recv_a, send_b, recv_b,
-    g, s1, r1, s2, r2, t, s3, r3, s4, r4, s5, r5,
-    lsem, gsem, sem_a, sem_b, rsem, fsem,
+    g, s1, r1, s2, r2, t, s3, r3, s4, r4, s5, rx, s6, r6, r5,
+    lsem, gsem, sem_a, sem_b, rsem, fsem, xsem, zsem,
 ):
     me, mp = lax.axis_index("dp"), lax.axis_index("mp")
     z, h, x = me // (NH * NX), (me // NX) % NH, me % NX
@@ -354,14 +354,26 @@
             c.wait_send()
         sum_h().wait_send()
 
-    def final(to, slot):
+    def rows_copy(src, dst, sems, out_slot, in_slot, to):
         return pltpu.make_async_remote_copy(
-            src_ref=s5.at[to], dst_ref=r5.at[slot],
-            send_sem=fsem.at[0, to], recv_sem=fsem.at[1, slot],
+            src_ref=src, dst_ref=dst, send_sem=sems.at[0, out_slot], recv_sem=sems.at[1, in_slot],
             device_id={"dp": to}, device_id_type=MESH,
         )
 
-    def send_final(hh):
+    def cross_x(to, slot):
+        return rows_copy(s5.at[0, to], rx.at[slot], xsem, to, slot, dp_of(z, h, to))
+
+    def cross_z(to, slot):
+        return rows_copy(s6.at[to], r6.at[slot], zsem, to, slot, dp_of(to, 1 - h, x))
+
+    def same(to, slot):
+        return rows_copy(
+            s5.at[1, to // NZ, to % NZ], r5.at[slot], fsem, to, slot, dp_of(to % NZ, h, to // NZ)
+        )
+
+    spot = x * NZ + z
+
+    def send_final(side, hh):
         low = lax.broadcasted_iota(jnp.int32, (NZ, NH * ROWS, BLK), 1) < ROWS
         for xx in range(NX):
             pair = []
@@ -371,14 +383,25 @@
                     pair.append(jnp.where(low, one, pltpu.roll(two, ROWS, 1)))
                 else:
                     pair.append(jnp.where(low, pltpu.roll(one, ROWS, 1), two))
-            rows = jnp.concatenate(pair, axis=1).astype(BF)
-            for zz in range(NZ):
-                s5[dp_of(zz, hh, xx)] = rows[zz]
-
-            @pl.loop(0, NZ)
-            def _(zz):
-                to = dp_of(zz, hh, xx)
-                pl.when(to != me)(lambda: final(to, me).start())
+            s5[side, xx] = jnp.concatenate(pair, axis=1).astype(BF)
+            if side == 0:
+                pl.when(x != xx)(lambda: cross_x(xx, x).start())
+            else:
+
+                @pl.loop(xx * NZ, (xx + 1) * NZ)
+                def _(to):
+                    pl.when(to != spot)(lambda: same(to, spot).start())
+
+    def cross_final():
+        acc = s5[0, x].astype(F32)
+        for k in (near, far, opp):
+            cross_x(k, k).wait_recv()
+            acc = acc + rx[k].astype(F32)
+        s6[...] = acc.astype(BF)
+
+        @pl.loop(0, NZ)
+        def _(to):
+            cross_z(to, z).start()
 
     reduce_x1()
 
@@ -409,10 +432,11 @@
 
         @pl.when(h == hh)
         def _():
-            send_final(1 - hh)
-            send_final(hh)
+            send_final(0, 1 - hh)
+            send_final(1, hh)
 
     token_grad(CHUNKS - 1)
+    cross_final()
     reduce_end()
 
     @pl.loop(0, CHUNKS)
@@ -421,19 +445,31 @@
             swap(send_a.at[c, mates[k]], recv_a.at[c, mp], sem_a, c, k).wait_send()
             swap(send_b.at[c, mates[k]], recv_b.at[c, mp], sem_b, c, k).wait_send()
 
-    def add_final(i, total):
-        peer = (me + i) % DP
-        final(peer, peer).wait_recv()
+    def add_same(i, total):
+        peer = (spot + i) % (NX * NZ)
+        same(peer, peer).wait_recv()
         return total + r5[peer].astype(F32)
 
-    total = lax.fori_loop(1, DP, add_final, s5[me].astype(F32)) * scale
+    def add_cross(i, total):
+        cross_z(i, i).wait_recv()
+        return total + r6[i].astype(F32)
+
+    total = lax.fori_loop(1, NX * NZ, add_same, s5[1, x, z].astype(F32))
+    total = lax.fori_loop(0, NZ, add_cross, total) * scale
     for b in range(LOC):
         gfirst_ref[b] = total[b * ROWS : (b + 1) * ROWS]
 
-    @pl.loop(1, DP)
+    for k in (near, far, opp):
+        cross_x(k, k).wait_send()
+
+    @pl.loop(0, NZ)
     def _(i):
-        peer = (me + i) % DP
-        final(peer, peer).wait_send()
+        cross_z(i, i).wait_send()
+
+    @pl.loop(1, NX * NZ)
+    def _(i):
+        peer = (spot + i) % (NX * NZ)
+        same(peer, peer).wait_send()
 
 
 def store_kernel(*refs):
@@ -507,14 +543,19 @@
             pltpu.VMEM((NZ - 1, LOC * slot, BLK), BF),
             pltpu.VMEM((LOC, ROWS, BLK), F32),
             pltpu.VMEM((LOC, ROWS, BLK), F32),
-            pltpu.VMEM((DP, LOC * ROWS, BLK), BF),
-            pltpu.VMEM((DP, LOC * ROWS, BLK), BF),
+            pltpu.VMEM((2, NX, NZ, LOC * ROWS, BLK), BF),
+            pltpu.VMEM((NX, NZ, LOC * ROWS, BLK), BF),
+            pltpu.VMEM((NZ, LOC * ROWS, BLK), BF),
+            pltpu.VMEM((NZ, LOC * ROWS, BLK), BF),
+            pltpu.VMEM((NX * NZ, LOC * ROWS, BLK), BF),
             dma((4,)),
             dma((3, 2, 14)),
             dma((2, CHUNKS, NM - 1)),
             dma((2, CHUNKS, NM - 1)),
             dma((2, 12)),
-            dma((2, DP)),
+            dma((2, NX * NZ)),
+            dma((2, NX)),
+            dma((2, NZ)),
         ],
         compiler_params=pltpu.CompilerParams(
             collective_id=0, has_side_effects=True, vmem_limit_bytes=40 * 1024 * 1024

time: 103 us -> 100 us (0.971)
  the two profiles are of different devices: /device:TPU:14 before, /device:TPU:16 now
where the time goes in v6:
time: 100 us; the launch traced here: 99.9 us
  Pallas kernels  99.2 us (99%)
    pallas_call x1, Pallas kernels, on_device(): pl.pallas_call(functools.partial(kernel, scale), out_shape=(jax.ShapeDtyp...  97.9 us

profile of v6, /device:TPU:16, one launch (start us, length us, event | category | flops | bytes accessed | tf_op | source)
XLA Modules:
  0.0 99.9 jit_solution(17972513105780692280)
XLA Ops:
  0.6 97.9 %monarch_layer.1 = (bf16[512,1024]{1,0:T(8,128)(2,1)S(1)}, bf16[512,1024]{1,0:T(8,128)(2,1)S(1)}, f32[4,4,256]{2,1,0:T(4,128)S(1)}, f32[4,4,256]{2,1,0:T(4,128)S(1)}) custom-call(bf16[512,1024]{1,0:T(8,128)(2,1)} %x_hbm.1, bf16[512,1024]{1,0:T(8,128)(2,1)} %up_hbm.1, bf16[4,4,256]{2,1,0:T(4,128)(2,1)} %first_hbm.1, bf16[4,4,256]{2,1,0:T(4,128)(2,1)} %second_hbm.1), custom_call_target="tpu_custom_call" | custom-call | tf_op jit(solution)/shard_map/monarch_layer/pallas_call | solution.py:507
  98.5 1.4 %store_results.1 = (bf16[512,1024]{1,0:T(8,128)(2,1)}, bf16[512,1024]{1,0:T(8,128)(2,1)}, f32[4,4,256]{2,1,0:T(4,128)}, f32[4,4,256]{2,1,0:T(4,128)}) custom-call(bf16[512,1024]{1,0:T(8,128)(2,1)S(1)} %get-tuple-element.8.refs_0_, bf16[512,1024]{1,0:T(8,128)(2,1)S(1)} %get-tuple-element.9.refs_1_, f32[4,4,256]{2,1,0:T(4,128)S(1)} %get-tuple-element.10.refs_2_, ...), custom_call_target="tpu_custom_call" | custom-call | tf_op jit(solution)/shard_map/store_results/pallas_call | solution.py:489

commit v7 on v6

--- a/solution.py
+++ b/solution.py
@@ -115,16 +115,20 @@
         part = bufs[f].at[x, z, h]
         return push(part, part, gsem.at[f], 0, to_y)
 
-    def gather_z(f):
-        part = bufs[f].at[x, z]
-        return [push(part, part, gsem.at[f], k, to_z[k - 1]) for k in range(1, NZ)]
-
-    def gather_x(f):
+    runs = ((0, h, 0), (0, 1 - h, 14), (1, None, 0), (2, None, 0))
+
+    def gather_z(run):
+        f, hh, base = run
+        part = bufs[f].at[x, z] if hh is None else bufs[f].at[x, z, hh]
+        return [push(part, part, gsem.at[f], base + k, to_z[k - 1]) for k in range(1, NZ)]
+
+    def gather_x(run):
+        f, hh, base = run
         halves = [pl.ds(0, HALF), pl.ds(HALF, HALF)]
 
         def one(slot, half, k, peer):
-            part = bufs[f].at[slot, halves[half]]
-            return push(part, part, gsem.at[f], k, peer)
+            part = bufs[f].at[slot, halves[half]] if hh is None else bufs[f].at[slot, halves[half], hh]
+            return push(part, part, gsem.at[f], base + k, peer)
 
         def first():
             return [one(x, 0, 8, to_near), one(x, 1, 9, to_far)]
@@ -137,18 +141,18 @@
 
         return first, second, relay
 
-    def open_x(f):
-        first, second, _ = gather_x(f)
+    def open_x(run):
+        first, second, _ = gather_x(run)
         start(first() + second())
 
-    def relay_x(f):
-        first, _, relay = gather_x(f)
+    def relay_x(run):
+        first, _, relay = gather_x(run)
         for c, onward in zip(first(), relay()):
             c.wait_recv()
             onward.start()
 
-    def close_x(f):
-        first, second, relay = gather_x(f)
+    def close_x(run):
+        first, second, relay = gather_x(run)
         rest = second() + relay()
         for c in rest:
             c.wait_recv()
@@ -188,24 +192,29 @@
             buf_a[0, x, z, h] = jnp.where(yl < NY // 2, high, low).astype(BF)
             buf_a[1, x, z, h] = jnp.where(yl < NY // 2, low, high).astype(BF)
     pl.semaphore_wait(barrier, 3 + len(to_z) + len(mates))
-    for f in range(3):
+    own, other, late, second_run = runs
+    gather_h(0).start()
+    start(gather_z(own))
+    for f in range(1, 3):
         gather_h(f).start()
     write_perm(p_x, natural_of_sorted)
     for f in range(3):
         gather_h(f).wait()
-        start(gather_z(f))
+        start(gather_z(runs[f + 1]))
+    write_perm(p_send, natural_of_send)
+    wait(gather_z(own))
+    open_x(own)
     write_perm(p_nat, natural_of_gathered)
-    write_perm(p_send, natural_of_send)
-    wait(gather_z(0))
-    open_x(0)
-    wait(gather_z(1))
+    relay_x(own)
+    wait(gather_z(other))
+    open_x(other)
+    wait(gather_z(late))
+    relay_x(other)
+    open_x(late)
     write_perm(p_sort, arrived_of_sorted)
-    relay_x(0)
-    open_x(1)
-    write_perm(p_srt, sorted_of_gathered)
-    g[...] = jnp.zeros_like(g)
     load_x.wait()
-    close_x(0)
+    close_x(own)
+    close_x(other)
 
     def side_lanes(p):
         return pl.ds(pl.multiple_of(sides[p] * 128, 128), 128)
@@ -241,10 +250,10 @@
 
     for p in range(2):
         if p == 1:
-            relay_x(1)
-            wait(gather_z(2))
-            open_x(2)
-            close_x(1)
+            relay_x(late)
+            wait(gather_z(second_run))
+            open_x(second_run)
+            close_x(late)
         sort_first(p)
         at = chunk(0)
         half = [nn(x_ref[at, block(b)], w1[b, :, side_lanes(p)]).astype(BF) for b in range(LOC)]
@@ -268,12 +277,14 @@
 
         @pl.when(c == 1)
         def _():
-            relay_x(2)
+            relay_x(second_run)
 
         sort_tokens(at)
 
     sort_tokens(chunk(0))
-    close_x(2)
+    close_x(second_run)
+    write_perm(p_srt, sorted_of_gathered)
+    g[...] = jnp.zeros_like(g)
     rows = buf_b[...].reshape(FEAT, BLK)
     for b in range(LOC):
         w2[b] = nn(p_srt[block(b), :], rows).astype(BF)
@@ -549,7 +560,7 @@
             pltpu.VMEM((NZ, LOC * ROWS, BLK), BF),
             pltpu.VMEM((NX * NZ, LOC * ROWS, BLK), BF),
             dma((4,)),
-            dma((3, 2, 14)),
+            dma((3, 2, 28)),
             dma((2, CHUNKS, NM - 1)),
             dma((2, CHUNKS, NM - 1)),
             dma((2, 12)),

time: 100 us -> 99.7 us (level)
  the two profiles are of different devices: /device:TPU:16 before, /device:TPU:8 now
where the time goes in v7:
time: 99.7 us; the launch traced here: 99.5 us
  Pallas kernels  98.9 us (99%)
    pallas_call x1, Pallas kernels, on_device(): pl.pallas_call(functools.partial(kernel, scale), out_shape=(jax.ShapeDtyp...  97.5 us

profile of v7, /device:TPU:8, one launch (start us, length us, event | category | flops | bytes accessed | tf_op | source)
XLA Modules:
  0.0 99.5 jit_solution(14415458829374961752)
XLA Ops:
  0.6 97.5 %monarch_layer.1 = (bf16[512,1024]{1,0:T(8,128)(2,1)S(1)}, bf16[512,1024]{1,0:T(8,128)(2,1)S(1)}, f32[4,4,256]{2,1,0:T(4,128)S(1)}, f32[4,4,256]{2,1,0:T(4,128)S(1)}) custom-call(bf16[512,1024]{1,0:T(8,128)(2,1)} %x_hbm.1, bf16[512,1024]{1,0:T(8,128)(2,1)} %up_hbm.1, bf16[4,4,256]{2,1,0:T(4,128)(2,1)} %first_hbm.1, bf16[4,4,256]{2,1,0:T(4,128)(2,1)} %second_hbm.1), custom_call_target="tpu_custom_call" | custom-call | tf_op jit(solution)/shard_map/monarch_layer/pallas_call | solution.py:518
  98.2 1.4 %store_results.1 = (bf16[512,1024]{1,0:T(8,128)(2,1)}, bf16[512,1024]{1,0:T(8,128)(2,1)}, f32[4,4,256]{2,1,0:T(4,128)}, f32[4,4,256]{2,1,0:T(4,128)}) custom-call(bf16[512,1024]{1,0:T(8,128)(2,1)S(1)} %get-tuple-element.8.refs_0_, bf16[512,1024]{1,0:T(8,128)(2,1)S(1)} %get-tuple-element.9.refs_1_, f32[4,4,256]{2,1,0:T(4,128)S(1)} %get-tuple-element.10.refs_2_, ...), custom_call_target="tpu_custom_call" | custom-call | tf_op jit(solution)/shard_map/store_results/pallas_call | solution.py:500
